TPU v7x, 128 devices: a whole 4x4x4 slice. The times are simulated.
128 devices in a mesh: layer: 32 (over x, z, core), batch: 4 (over y).
Axes of the slice: x: 4, y: 4, z: 4, core: 2. Of those that a mesh axis runs over, the one named last changes fastest.
Arguments:
- first_state: float32 [4, 32, 32, 256], P('batch'), may hold values from -6 to 6
- guess_points: float32 [32, 4, 32, 32, 256], P('layer', 'batch'), may hold values from -6 to 6
- weights: bfloat16 [128, 3, 3, 256, 256], P('layer'), may hold values from -0.5 to 0.5
Outputs:
- states: float32 [128, 4, 32, 32, 256], P('layer', 'batch')
- norms: float32 [32], P('layer')
All inputs are finite; a program needn't handle non-finite values.
Results may differ from a plain program's by a relative error of at most 0.0038.
Values sent between devices are 32-bit elements; how exact they have to be, the bound alone decides.
No kernel may reach another device: no remote copies, remote signals or barrier semaphores. Data moves between devices by JAX's collectives and lax.ppermute only.
A program may use at most 128 MiB of HBM per device.

v0:
```python
import jax
import jax.numpy as jnp
from jax import lax
from jax.experimental import pallas as pl
from jax.experimental.pallas import tpu as pltpu
from jax.sharding import PartitionSpec as P


CH = 256
SIDE = 32
ROWS = SIDE * SIDE
TAPS = 9 * CH
TILE = 256
H = 2.0 / 128
STATE = jax.ShapeDtypeStruct((ROWS, CH), jnp.float32)
ANY = pl.BlockSpec(memory_space=pl.ANY)
HBM = pl.BlockSpec(memory_space=pltpu.HBM)
VMEM = pl.BlockSpec(memory_space=pltpu.VMEM)


def stencil_put(buf, r, value):
    rows = value.shape[0]
    cube = value.reshape(rows // SIDE, SIDE, CH)
    column = lax.broadcasted_iota(jnp.int32, (1, SIDE, CH), 1)
    before = jnp.where(column == 0, 0.0, pltpu.roll(cube, 1, 1)).reshape(rows, CH)
    behind = jnp.where(column == SIDE - 1, 0.0, pltpu.roll(cube, SIDE - 1, 1)).reshape(rows, CH)
    at = pl.ds(SIDE + r, rows)
    buf[at, 0:CH] = before.astype(jnp.bfloat16)
    buf[at, CH : 2 * CH] = value.astype(jnp.bfloat16)
    buf[at, 2 * CH : 3 * CH] = behind.astype(jnp.bfloat16)


def stencil_pads(*bufs):
    zero = jnp.zeros((SIDE, 3 * CH), jnp.bfloat16)
    for buf in bufs:
        buf[0:SIDE, :] = zero
        buf[SIDE + ROWS :, :] = zero


def relu_conv(buf, weight, r):
    total = None
    for dy in range(3):
        part = jnp.dot(
            buf[pl.ds(r + SIDE * dy, TILE), :],
            weight[pl.ds(3 * CH * dy, 3 * CH), :],
            preferred_element_type=jnp.float32,
        )
        total = part if total is None else total + part
    return jnp.maximum(total, 0.0)


def run_steps(start, bufs, held, steps):
    @pl.loop(0, ROWS // TILE)
    def _(i):
        r = pl.multiple_of(i * TILE, TILE)
        stencil_put(bufs[0], r, start(r))

    for n, (ready, weight, update) in enumerate(steps):
        ready()
        source, target = bufs[n % 2], bufs[(n + 1) % 2]
        for r in range(0, ROWS, TILE):
            current = start(r) if n == 0 else held[r : r + TILE, :]
            value = update(r, current, relu_conv(source, weight, r))
            if n + 1 < len(steps):
                held[r : r + TILE, :] = value
                stencil_put(target, r, value)


def run_pairs(start, bufs, held, copies, weights, update):
    @pl.loop(0, ROWS // TILE)
    def _(i):
        r = pl.multiple_of(i * TILE, TILE)
        value = start(r)
        held[pl.ds(r, TILE), :] = value
        stencil_put(bufs[0], r, value)

    @pl.loop(0, 2)
    def _(turn):
        for slot in range(2):
            copies(2 * turn + slot).wait()
            for r in range(0, ROWS, TILE):
                a = relu_conv(bufs[slot], weights.at[2 * turn + slot], r)
                value = update(turn, slot, r, held[r : r + TILE, :], a)
                held[r : r + TILE, :] = value
                stencil_put(bufs[1 - slot], r, value)


SCRATCH = (
    pltpu.VMEM((ROWS + 2 * SIDE, 3 * CH), jnp.bfloat16),
    pltpu.VMEM((ROWS + 2 * SIDE, 3 * CH), jnp.bfloat16),
    pltpu.VMEM((ROWS, CH), jnp.float32),
)


class Load:
    def __init__(self, choices, target, sem):
        self.choices, self.target, self.sem = choices, target, sem

    def start(self):
        for condition, source in self.choices:
            if condition is None:
                pltpu.make_async_copy(source, self.target, self.sem).start()
                continue

            @pl.when(condition)
            def _(source=source):
                pltpu.make_async_copy(source, self.target, self.sem).start()

    def wait(self):
        pltpu.make_async_copy(self.choices[0][1], self.target, self.sem).wait()


def plain(source, target, sem):
    return Load([(None, source)], target, sem)


def start_all(*loads):
    for load in loads:
        load.start()


def wait_all(*loads):
    for load in loads:
        load.wait()


def rows(ref):
    return lambda r: ref[pl.ds(r, TILE), :]


def either(condition, yes, no):
    return lambda r: jnp.where(condition, yes[pl.ds(r, TILE), :], no[pl.ds(r, TILE), :])


def ready(waits, starts=()):
    def run():
        wait_all(*waits)
        start_all(*starts)

    return run


def spot():
    d = lax.axis_index("layer")
    return d, d // 8, (d // 2) % 4, d % 2


def nothing():
    return None


def kernel_call(body, outs, out_specs, args, in_specs, scratch, convs, grant, aliases=None):
    return pl.pallas_call(
        body,
        out_shape=outs,
        in_specs=in_specs,
        out_specs=out_specs,
        scratch_shapes=scratch,
        input_output_aliases=aliases or {},
        compiler_params=pltpu.CompilerParams(vmem_limit_bytes=grant << 20),
        cost_estimate=pl.CostEstimate(flops=convs * 2 * ROWS * TAPS * CH, bytes_accessed=4 << 20, transcendentals=0),
    )(*args)


def room(n):
    return [pltpu.VMEM((n, ROWS, CH), jnp.float32), pltpu.SemaphoreType.DMA((n,))]


def wbuf(n):
    return [pltpu.VMEM((n, TAPS, CH), jnp.bfloat16), pltpu.SemaphoreType.DMA((n,))]


def sweep_body(first, given, w, out, b0, b1, wv, ws):
    x = either(lax.axis_index("layer") == 0, first, given)

    def copies(n):
        return pltpu.make_async_copy(w.at[n], wv.at[n], ws.at[n])

    start_all(*(copies(n) for n in range(4)))
    stencil_pads(b0, b1)
    run_pairs(x, (b0, b1), out, copies, wv, lambda turn, slot, r, v, a: v + H * a)


def sweep(first, given, w):
    return kernel_call(sweep_body, STATE, VMEM, (first, given, w), [VMEM, VMEM, HBM], [*SCRATCH[:2], *wbuf(4)], 4, 16)


def resweep_body(first, given, w, relaxed, fine, send, squares, b0, b1, held, ahead, sums, wv, ws):
    d = lax.axis_index("layer")
    x = either(d == 0, first, given)

    def copies(n):
        return pltpu.make_async_copy(w.at[n], wv.at[n], ws.at[n])

    start_all(*(copies(n) for n in range(4)))
    stencil_pads(b0, b1)
    sums[...] = jnp.zeros_like(sums)

    def update(turn, slot, r, v, a):
        value = v + H * a
        at = slice(r, r + TILE)
        if slot == 0:
            ahead[turn, at, :] = v + 4 * H * a
            return value
        rhs = value - ahead[0, at, :]
        fine[at, :] = rhs
        off = value - relaxed[at, :]
        sums[turn] += jnp.sum((off * off).reshape(TILE // 8, 8, CH), axis=0)
        send[at, :] = jnp.where(d % 4 < 2, value, rhs)
        return value

    run_pairs(x, (b0, b1), held, copies, wv, update)
    squares[...] = sums[1]


def resweep(first, given, w, relaxed):
    return kernel_call(
        resweep_body, (STATE, STATE, jax.ShapeDtypeStruct((8, CH), jnp.float32)), (VMEM,) * 3,
        (first, given, w, relaxed), [VMEM, VMEM, HBM, VMEM],
        [*SCRATCH, pltpu.VMEM((2, ROWS, CH), jnp.float32), pltpu.VMEM((2, 8, CH), jnp.float32), *wbuf(4)], 4,
        20,
    )


def coarse_update(rhs):
    return lambda r, v, a: v + 4 * H * a + rhs[r : r + TILE, :]


def coarse_last(rhs, out):
    def update(r, v, a):
        out[r : r + TILE, :] = v + 4 * H * a + rhs[r : r + TILE, :]

    return update


def one_coarse_body(x, w, rhs, out, b0, b1, held, fv, fs, wv, ws):
    ww = plain(w.at[0], wv.at[0], ws.at[0])
    ff = plain(rhs, fv.at[0], fs.at[0])
    start_all(ww, ff)
    stencil_pads(b0, b1)
    run_steps(rows(x), (b0, b1), held, [(ready([ww, ff]), wv.at[0], coarse_last(fv.at[0], out))])


def one_coarse(x, w, rhs):
    return kernel_call(
        one_coarse_body, STATE, VMEM, (x, w, rhs), [VMEM, HBM, ANY], [*SCRATCH, *room(1), *wbuf(1)], 1,
        14,
    )


def two_coarse_body(x, wa, w, rhs_a, rhs_b, out, b0, b1, held, fv, fs, wv, ws):
    ww = [plain(wa, wv.at[0], ws.at[0]), plain(w.at[0], wv.at[1], ws.at[1])]
    ff = [plain(rhs_a, fv.at[0], fs.at[0]), plain(rhs_b, fv.at[1], fs.at[1])]
    start_all(ww[0], ff[0])
    stencil_pads(b0, b1)
    run_steps(
        rows(x), (b0, b1), held,
        [(ready([ww[0], ff[0]], [ww[1], ff[1]]), wv.at[0], coarse_update(fv.at[0])),
         (ready([ww[1], ff[1]]), wv.at[1], coarse_last(fv.at[1], out))],
    )


def two_coarse(x, wa, w, rhs_a, rhs_b):
    return kernel_call(
        two_coarse_body, STATE, VMEM, (x, wa, w, rhs_a, rhs_b), [VMEM, ANY, HBM, ANY, ANY],
        [*SCRATCH, *room(2), *wbuf(2)], 2, 16,
    )


def group_body(first, ends, w0, w1, w2, w3, f0, f1, f2, f3, out, b0, b1, held, ahead, fv, fs, wv, ws):
    d = lax.axis_index("layer")
    x = either(d == 1, first, ends)
    ww = [plain(s, wv.at[n], ws.at[n]) for n, s in enumerate((w0, w1.at[0], w2, w3))]
    ff = [plain(s, fv.at[n], fs.at[n]) for n, s in enumerate((f0, f1, f2, f3))]
    for n in range(4):
        start_all(ww[n], ff[n])
    stencil_pads(b0, b1)

    class copies:
        def __init__(self, n):
            self.n = n

        def wait(self):
            pltpu.make_async_copy(w0, wv.at[self.n], ws.at[self.n]).wait()
            pltpu.make_async_copy(f0, fv.at[self.n], fs.at[self.n]).wait()

    def update(turn, slot, r, v, a):
        at = slice(r, r + TILE)
        value = v + 4 * H * a + fv[2 * turn + slot, at, :]
        if slot == 0:
            ahead[turn, at, :] = v + 16 * H * a
        else:
            out[at, :] = jnp.where(d == 5, value, value - ahead[0, at, :])
        return value

    run_pairs(x, (b0, b1), held, copies, wv, update)


def group(*args):
    return kernel_call(
        group_body, STATE, VMEM, args, [VMEM, VMEM, ANY, HBM] + [ANY] * 6,
        [*SCRATCH, pltpu.VMEM((2, ROWS, CH), jnp.float32), *room(4), *wbuf(4)], 4, 22,
    )


def relay_body(came2, came3, rhs2, rhs3, we2, we3, w02, w03, own2, own3, ca, cb, b0, b1, held, wv, ws):
    _, _, z, _ = spot()
    third = z == 3
    other = z != 3
    x, ra, rb = either(third, came3, came2), either(third, rhs3, rhs2), either(third, own3, own2)
    got_wa = Load([(third, we3), (other, we2)], wv.at[0], ws.at[0])
    got_wb = Load([(third, w03), (other, w02)], wv.at[1], ws.at[1])
    start_all(got_wa, got_wb)
    stencil_pads(b0, b1)

    def first(r, v, a):
        value = v + 16 * H * a + ra(r)
        ca[r : r + TILE, :] = value
        return value

    def second(r, v, a):
        cb[r : r + TILE, :] = v + 16 * H * a + rb(r)

    run_steps(
        x, (b0, b1), held, [(ready([got_wa]), wv.at[0], first), (ready([got_wb]), wv.at[1], second)]
    )


def relay(*args):
    return kernel_call(
        relay_body, (STATE, STATE), (VMEM, VMEM), args, [VMEM] * 4 + [ANY] * 4 + [VMEM] * 2, [*SCRATCH, *wbuf(2)], 2,
        16,
    )


def choose_body(ends, made, got, cb1, cb2, out, sem):
    _, x, z, _ = spot()
    load = Load([((x == 0) & (z < 2), ends), ((x == 0) & (z == 2), made), ((x == 0) & (z == 3), got),
                 (x == 1, cb1), (x >= 2, cb2)], out, sem)
    load.start()
    load.wait()


def choose(*args):
    return kernel_call(choose_body, STATE, VMEM, args, [ANY] * 5, [pltpu.SemaphoreType.DMA], 0, 8)


def correct_body(first, ends_in, even_in, ca1, ca2, came, rhs2, rhs3, we2, we3, wa0, wb0, wa1, wb1,
                 fa0, fb0, fa1, fb1, made, got, ends, send, move, coarse, b0, b1, held, xv, xs, wv, ws):
    d, xc, z, _ = spot()
    is_a = z % 2 == 0
    is_b = z % 2 == 1
    odd = z >= 2
    third = z == 3
    other = z != 3
    late = (xc == 3) & odd
    x, ra, g0, g1, rk = (xv.at[n] for n in range(5))
    got_x = Load(
        [((xc == 0) & (z < 2), first), ((xc == 0) & (z == 2), ends_in),
         (((xc == 0) & third) | ((xc > 0) & (z < 2)), even_in),
         ((xc == 1) & odd, ca1), ((xc == 2) & odd, ca2), (late, came)], x, xs.at[0])
    got_e = Load([(third, we3), (other, we2)], wv.at[0], ws.at[0])
    got_ra = Load([(third, rhs3), (other, rhs2)], ra, xs.at[1])
    got_w0 = Load([(is_a, wa0), (is_b, wb0)], wv.at[1], ws.at[1])
    got_w1 = Load([(is_a, wa1.at[0]), (is_b, wb1)], wv.at[2], ws.at[2])
    got_f0 = Load([(is_a, fa0), (is_b, fb0)], g0, xs.at[2])
    got_f1 = Load([(is_a, fa1), (is_b, fb1)], g1, xs.at[3])
    got_r = Load([(is_a, made), (is_b & (d // 4 > 0), got), (is_b & (d // 4 == 0), ends)], rk, xs.at[4])
    start_all(got_x, got_e, got_ra)
    stencil_pads(b0, b1)
    got_x.wait()
    wait_all(got_e, got_ra)
    start_all(got_w0, got_f0, got_r, got_w1, got_f1)

    @pl.when(late)
    def _():
        def update(r, v, a):
            held[r : r + TILE, :] = v + 16 * H * a + ra[r : r + TILE, :]

        run_steps(rows(x), (b0, b1), held, [(nothing, wv.at[0], update)])
        x[...] = held[...]

    def zero(r, v, a):
        rk_rows = rk[r : r + TILE, :]
        coarse[r : r + TILE, :] = jnp.where(d // 4 < 2, rk_rows, v + 16 * H * a + rk_rows)
        value = v + 4 * H * a + g0[r : r + TILE, :]
        move[r : r + TILE, :] = value
        send[r : r + TILE, :] = v
        return value

    def one(r, v, a):
        @pl.when(is_b)
        def _():
            value = v + 4 * H * a + g1[r : r + TILE, :]
            move[r : r + TILE, :] = value
            send[r : r + TILE, :] = value

    run_steps(
        rows(x), (b0, b1), held,
        [(ready([got_w0, got_f0, got_r]), wv.at[1], zero), (ready([got_w1, got_f1]), wv.at[2], one)],
    )


def correct(*args):
    return kernel_call(
        correct_body, (STATE,) * 3, (VMEM,) * 3, args, [ANY] * 12 + [HBM] + [ANY] * 8,
        [*SCRATCH, *room(5), *wbuf(3)], 3, 22
    )


def second_body(x, w2, f2, out, b0, b1, held, wv, ws):
    _, _, z, core = spot()

    @pl.when((core == 1) & (z % 2 == 1))
    def _():
        got = plain(w2, wv.at[0], ws.at[0])
        got.start()
        stencil_pads(b0, b1)
        run_steps(rows(x), (b0, b1), held, [(ready([got]), wv.at[0], coarse_last(f2, out))])


def second(x, w2, f2):
    return kernel_call(second_body, STATE, VMEM, (x, w2, f2), [VMEM, ANY, VMEM], [*SCRATCH, *wbuf(1)], 1, 12)


def finish_body(x0, xa, xb, coarse, w, rhs, out, b0, b1, held, wv, ws, stage, os):
    _, _, z, core = spot()
    is_b = z % 2 == 1
    last = (core == 1) & is_b
    ww = [plain(w.at[n], wv.at[n], ws.at[n]) for n in range(3)]
    start_all(*ww)
    stencil_pads(b0, b1)

    @pl.loop(0, ROWS // TILE)
    def _(i):
        r = pl.multiple_of(i * TILE, TILE)
        at = pl.ds(r, TILE)
        value = jnp.where(core == 0, x0[at, :], jnp.where(is_b, xb[at, :], xa[at, :]))
        held[at, :] = value
        stencil_put(b0, r, value)

    ww[0].wait()
    for r in range(0, ROWS, TILE):
        at = slice(r, r + TILE)
        a = relu_conv(b0, wv.at[0], r)
        v = held[at, :]
        stage[3, at, :] = jnp.where(last, coarse[at, :], v + 4 * H * a + rhs[at, :])
        value = v + H * a
        stage[0, at, :] = value
        stencil_put(b1, r, value)
    pltpu.make_async_copy(stage.at[0], out.at[0], os.at[0]).start()
    pltpu.make_async_copy(stage.at[3], out.at[3], os.at[3]).start()
    for n, source, target in ((1, b1, b0), (2, b0, b1)):
        ww[n].wait()
        for r in range(0, ROWS, TILE):
            at = slice(r, r + TILE)
            value = stage[n - 1, at, :] + H * relu_conv(source, wv.at[n], r)
            stage[n, at, :] = value
            if n == 1:
                stencil_put(target, r, value)
        pltpu.make_async_copy(stage.at[n], out.at[n], os.at[n]).start()
    for n in range(4):
        pltpu.make_async_copy(stage.at[n], out.at[n], os.at[n]).wait()


OUT = jax.ShapeDtypeStruct((4, ROWS, CH), jnp.float32)


def finish(*args):
    return kernel_call(
        finish_body, OUT, ANY, args, [VMEM] * 4 + [HBM, VMEM],
        [*SCRATCH, *wbuf(3), pltpu.VMEM((4, ROWS, CH), jnp.float32), pltpu.SemaphoreType.DMA((4,))], 3, 22,
    )


def widen_body(w, out, wv, sem):
    load = plain(w.at[0], wv, sem)
    load.start()
    load.wait()

    @pl.loop(0, TAPS // TILE)
    def _(n):
        at = pl.ds(pl.multiple_of(n * TILE, TILE), TILE)
        out[at, :] = wv[at, :].astype(jnp.float32)


def widen(w):
    return kernel_call(
        widen_body, jax.ShapeDtypeStruct((TAPS, CH), jnp.float32), VMEM, (w,), [HBM],
        [pltpu.VMEM((TAPS, CH), jnp.bfloat16), pltpu.SemaphoreType.DMA], 0, 8,
    )


def norm_sum_body(a, b, out):
    out[...] = a[...] + b[...]


def norm_sum(a, b):
    return kernel_call(norm_sum_body, jax.ShapeDtypeStruct((8, CH), jnp.float32), VMEM, (a, b), [VMEM, VMEM], [], 0, 2)


def norm_root_body(a, b, out):
    total = jnp.sum(a[...] + b[...])
    root = jnp.sqrt(jnp.full((8, 128), total, jnp.float32) / (4 * ROWS * CH) + 1e-06)
    out[0] = jnp.max(root)


def norm_root(a, b):
    return kernel_call(
        norm_root_body, jax.ShapeDtypeStruct((1,), jnp.float32), pl.BlockSpec(memory_space=pltpu.SMEM), (a, b),
        [VMEM, VMEM], [], 0, 2,
    )


def narrow_body(x, out):
    @pl.loop(0, TAPS // TILE)
    def _(n):
        at = pl.ds(pl.multiple_of(n * TILE, TILE), TILE)
        out[at, :] = x[at, :].astype(jnp.bfloat16)


def narrow(x):
    return kernel_call(narrow_body, jax.ShapeDtypeStruct((TAPS, CH), jnp.bfloat16), VMEM, (x,), [VMEM], [], 0, 8)


PART = TAPS // 4


def pack_body(chip, own, narrowed, out):
    start = lax.axis_index("batch") * PART

    @pl.loop(0, TAPS // TILE)
    def _(n):
        at = pl.ds(pl.multiple_of(n * TILE, TILE), TILE)
        narrowed[at, :] = chip[at, :].astype(jnp.bfloat16)

    @pl.loop(0, PART // 64)
    def _(n):
        at = pl.ds(pl.multiple_of(start + n * 64, 64), 64)
        out[pl.ds(pl.multiple_of(n * 64, 64), 64), :] = chip[at, :]
        out[pl.ds(pl.multiple_of(PART + n * 64, 64), 64), :] = own[at, :]


def pack(chip, own):
    return kernel_call(
        pack_body, (jax.ShapeDtypeStruct((TAPS, CH), jnp.bfloat16), jax.ShapeDtypeStruct((2 * PART, CH), jnp.float32)),
        (VMEM, VMEM), (chip, own), [VMEM, VMEM], [], 0, 8,
    )


def unpack_body(p0, p1, p2, p3, out0, out1):
    y = lax.axis_index("batch")
    for n, part in enumerate((p0, p1, p2, p3)):
        start = (y + 4 - n) % 4 * PART

        @pl.loop(0, PART // 64)
        def _(i, part=part, start=start):
            at = pl.ds(pl.multiple_of(start + i * 64, 64), 64)
            out0[at, :] = part[pl.ds(pl.multiple_of(i * 64, 64), 64), :].astype(jnp.bfloat16)
            out1[at, :] = part[pl.ds(pl.multiple_of(PART + i * 64, 64), 64), :].astype(jnp.bfloat16)


def unpack(*parts):
    kernel = jax.ShapeDtypeStruct((TAPS, CH), jnp.bfloat16)
    return kernel_call(unpack_body, (kernel, kernel), (VMEM, VMEM), parts, [VMEM] * 4, [], 0, 10)


def send(value, pairs, axis="layer"):
    return lax.ppermute(value, axis, pairs)


A0 = [4 * k for k in range(8)]


def cycle(first_state, guess_points, weights):
    first = first_state.reshape(ROWS, CH)
    guess = guess_points.reshape(ROWS, CH)
    w = weights.reshape(4, TAPS, CH)
    shift = [(i, i + 1) for i in range(31)]

    came = send(guess, shift)
    wide = widen(w)
    w_chip = send(wide, [p for k in A0 for p in ((k, k + 1), (k + 2, k + 3))])
    w_z2 = send(wide, [(k + 2, k + 1) for k in A0])
    wn_chip, packed = pack(w_chip, wide)
    part0 = send(packed, [(k + 1, k + 3) for k in A0])
    relaxed = sweep(first, came, w)

    came = send(relaxed, shift)
    w_z3 = send(wide, [(k + 3, k + 1) for k in A0] + [(8 * x, 8 * x + 7) for x in range(1, 4)])
    fine, out0, squares = resweep(first, came, w, relaxed)

    in0 = send(out0, [p for k in A0 for p in ((k, k + 1), (k + 2, k + 3))])
    q1 = one_coarse(in0, w, fine)
    came = send(q1, [(k + 1, k + 3) for k in A0])
    fine_3 = send(fine, [p for k in A0 for p in ((k + 3, k + 1), (k + 1, k + 3))])
    fine_a0 = send(fine, [(k, k + 1) for k in A0])
    ends = two_coarse(came, wn_chip, w, in0, fine)

    ends_in = send(ends, [(k + 3, k + 5) for k in A0[:-1]])
    fine_2 = send(fine, [p for k in A0 for p in ((k + 2, k + 1), (k, k + 3))])
    parts = [part0]
    for n in (1, 2, 3):
        ring = [((k + 3) * 4 + y, (k + 3) * 4 + (y + n) % 4) for k in A0 for y in range(4)]
        parts.append(send(part0, ring, ("layer", "batch")))
    wn_z2, wn_z3 = narrow(w_z2), narrow(w_z3)
    w_even2 = send(w_z3, [(8 * x + 7, 8 * x + 5) for x in range(1, 4)])
    made = group(first, ends_in, wn_chip, w, wn_z2, wn_z3, fine_a0, fine, fine_2, fine_3)

    in_a = send(made, [(5, 13), (9, 15), (17, 23), (25, 31)])
    in_b = send(made, [(5, 15), (9, 13), (17, 21), (25, 29)])
    got = send(made, [(k + 1, k + 3) for k in A0])
    wn_even2 = narrow(w_even2)
    wn_b0, wn_b1 = unpack(*parts)

    common = (in_b, in_a, wn_even2, wn_z3, wn_chip, wn_b0, made, got)
    ca1, cb1 = relay(in_a, in_b, *common)
    came = send(cb1, [(13, 21), (15, 23)])
    swapped = send(squares, [(0, 1), (1, 0), (2, 3), (3, 2)], "batch")
    squares = norm_sum(squares, swapped)
    swapped = send(squares, [(0, 2), (2, 0), (1, 3), (3, 1)], "batch")
    norms = norm_root(squares, swapped)
    ca2, cb2 = relay(came, came, *common)
    came = send(cb2, [(21, 29), (23, 31)])
    carry = choose(ends, made, got, cb1, cb2)
    even_in = send(carry, [(3, 7), (5, 11), (7, 9), (13, 19), (15, 17), (21, 27), (23, 25)])
    out1, move, coarse = correct(
        first, ends_in, even_in, ca1, ca2, came, in_b, in_a, wn_even2, wn_z3, wn_chip, wn_b0, w, wn_b1,
        fine_a0, fine_2, fine, fine_3, made, got, ends,
    )
    in1 = send(out1, [p for k in A0 for p in ((k + 1, k), (k + 3, k + 2))])
    moved = second(move, wn_chip, in0)
    states = finish(in1, move, moved, coarse, w, fine)
    return states.reshape(4, 1, SIDE, SIDE, CH), norms


def solution(mesh):
    placed = (
        P("batch", None, None, None),
        P("layer", "batch", None, None, None),
        P("layer", None, None, None, None),
    )
    return jax.shard_map(
        cycle,
        mesh=mesh,
        in_specs=placed,
        out_specs=(P("layer", "batch", None, None, None), P("layer")),
        check_vma=False,
    )
```

profile of v0, /device:TPU:119, one launch (start us, length us, event | category | flops | bytes accessed | tf_op | source)
XLA Modules:
  0.0 233.8 jit_solution(8033856090577351495)
XLA Ops:
  1.9 3.6 %collective-permute-done.given = f32[1024,256]{1,0:T(8,128)S(1)} collective-permute-done((f32[1024,256]{1,0:T(8,128)}, f32[1024,256]{1,0:T(8,128)S(1)}, u32[]{:S(2)}, u32[]{:S(2)}) %collective-permute-start) | collective-permute-done | bytes 1048608 | tf_op jit(solution)/shard_map/ppermute | solution.py:569
  5.6 2.3 copy-done
  9.1 7.4 %shard_map.50.relaxed = f32[1024,256]{1,0:T(8,128)S(1)} custom-call(f32[1024,256]{1,0:T(8,128)S(1)} %bitcast.14, f32[1024,256]{1,0:T(8,128)S(1)} %collective-permute-done.given, bf16[4,2304,256]{2,1,0:T(8,128)(2,1)S(1)} %bitcast.6), custom_call_target="tpu_custom_call" | custom-call | flops 4831838208 | bytes 4194304 | tf_op jit(solution)/shard_map/pallas_call | solution.py:153
  18.6 15.9 %collective-permute-start.7 = (f32[2304,256]{1,0:T(8,128)S(1)}, f32[2304,256]{1,0:T(8,128)S(1)}, u32[]{:S(2)}, u32[]{:S(2)}) collective-permute-start(f32[2304,256]{1,0:T(8,128)S(1)} %shard_map.53.own), channel_id=1, source_target_pairs={{12,4},{28,20},{44,36},{60,52},{76,68},{92,84},{108,100},{124,116}... | collective-permute-start | bytes 7077896 | tf_op jit(solution)/shard_map/ppermute | solution.py:569
  35.9 8.1 %shard_map.51 = (f32[1024,256]{1,0:T(8,128)S(1)}, f32[1024,256]{1,0:T(8,128)S(1)}, f32[8,256]{1,0:T(8,128)S(1)}) custom-call(f32[1024,256]{1,0:T(8,128)S(1)} %bitcast.15, f32[1024,256]{1,0:T(8,128)S(1)} %collective-permute-done.1.given, bf16[4,2304,256]{2,1,0:T(8,128)(2,1)S(1)} %bitcast.8, f32[1024,256]{1,0:T(8,128)S(1)} %shard_map.50.relaxed), custom_call_target="tpu_custom_call" | custom-call | flops 4831838208 | bytes 4194304 | tf_op jit(solution)/shard_map/pallas_call | solution.py:153
  46.1 10.5 %collective-permute-done.2.x.rhs_a.f2 = f32[1024,256]{1,0:T(8,128)S(1)} collective-permute-done((f32[1024,256]{1,0:T(8,128)S(1)}, f32[1024,256]{1,0:T(8,128)S(1)}, u32[]{:S(2)}, u32[]{:S(2)}) %collective-permute-start.2) | collective-permute-done | bytes 1048608 | tf_op jit(solution)/shard_map/ppermute | solution.py:569
  59.8 4.1 %collective-permute-start.10 = (f32[1024,256]{1,0:T(8,128)S(1)}, f32[1024,256]{1,0:T(8,128)S(1)}, u32[]{:S(2)}, u32[]{:S(2)}) collective-permute-start(f32[1024,256]{1,0:T(8,128)S(1)} %get-tuple-element.17.rhs.rhs_b.f1.fa1), channel_id=1, source_target_pairs={{12,4},{4,12},{28,20},{20,28},{44,36},{36,44},{60,52},{52,60},{76,... | collective-permute-start | bytes 3145736 | tf_op jit(solution)/shard_map/ppermute | solution.py:569
  64.2 4.0 %collective-permute-start.14 = (f32[2304,256]{1,0:T(8,128)S(1)}, f32[2304,256]{1,0:T(8,128)S(1)}, u32[]{:S(2)}, u32[]{:S(2)}) collective-permute-start(f32[2304,256]{1,0:T(8,128)S(1)} %collective-permute-done.7.x), channel_id=1, source_target_pairs={{60,52},{92,84},{124,116},{61,53},{93,85},{125,117},{62,54},{94,86... | collective-permute-start | bytes 7077896 | tf_op jit(solution)/shard_map/ppermute | solution.py:569
  69.7 4.3 %collective-permute-done.3.x = f32[1024,256]{1,0:T(8,128)S(1)} collective-permute-done((f32[1024,256]{1,0:T(8,128)S(1)}, f32[1024,256]{1,0:T(8,128)S(1)}, u32[]{:S(2)}, u32[]{:S(2)}) %collective-permute-start.3) | collective-permute-done | bytes 1048608 | tf_op jit(solution)/shard_map/ppermute | solution.py:569
  75.3 3.9 %shard_map.55.ends = f32[1024,256]{1,0:T(8,128)S(1)} custom-call(f32[1024,256]{1,0:T(8,128)S(1)} %collective-permute-done.3.x, bf16[2304,256]{1,0:T(8,128)(2,1)S(1)} %get-tuple-element.18.wa.w0.w02.wa0.w2, bf16[4,2304,256]{2,1,0:T(8,128)(2,1)S(1)} %bitcast.10, f32[1024,256]{1,0:T(8,128)S(1)} %collective-permute-done.2.x.rhs_a.f2, ...), custom_call_target="tpu_custom_call" | custom-call | flops 2415919104 | bytes 4194304 | tf_op jit(solution)/shard_map/pallas_call | solution.py:153
  80.0 11.7 %collective-permute-done.10.f3.fb1 = f32[1024,256]{1,0:T(8,128)S(1)} collective-permute-done((f32[1024,256]{1,0:T(8,128)S(1)}, f32[1024,256]{1,0:T(8,128)S(1)}, u32[]{:S(2)}, u32[]{:S(2)}) %collective-permute-start.10) | collective-permute-done | bytes 1048608 | tf_op jit(solution)/shard_map/ppermute | solution.py:569
  92.4 16.8 %collective-permute-done.15.p0 = f32[1152,256]{1,0:T(8,128)S(1)} collective-permute-done((f32[1152,256]{1,0:T(8,128)S(1)}, f32[1152,256]{1,0:T(8,128)S(1)}, u32[]{:S(2)}, u32[]{:S(2)}) %collective-permute-start.15) | collective-permute-done | bytes 1179680 | tf_op jit(solution)/shard_map/ppermute | solution.py:569
  109.2 2.1 collective-permute-start.18
  111.6 4.7 %collective-permute-start.17 = (f32[1152,256]{1,0:T(8,128)S(1)}, f32[1152,256]{1,0:T(8,128)S(1)}, u32[]{:S(2)}, u32[]{:S(2)}) collective-permute-start(f32[1152,256]{1,0:T(8,128)S(1)} %collective-permute-done.15.p0), channel_id=1, source_target_pairs={{12,14},{13,15},{14,12},{15,13},{28,30},{29,31},{30,28},{31,29},{4... | collective-permute-start | bytes 3538952 | tf_op jit(solution)/shard_map/ppermute | solution.py:569
  118.2 8.2 %shard_map.58.own2.made = f32[1024,256]{1,0:T(8,128)S(1)} custom-call(f32[1024,256]{1,0:T(8,128)S(1)} %bitcast.16, f32[1024,256]{1,0:T(8,128)S(1)} %collective-permute-done.5.ends.ends_in, bf16[2304,256]{1,0:T(8,128)(2,1)S(1)} %get-tuple-element.18.wa.w0.w02.wa0.w2, bf16[4,2304,256]{2,1,0:T(8,128)(2,1)S(1)} %bitcast.11, bf16[2304,256]{1,0:T(8,128)(2,1)S(1)} %shard_map.56.w2, ...), custom_call_target="tpu_custom_call" | custom-call | flops 4831838208 | bytes 4194304 | tf_op jit(solution)/shard_map/pallas_call | solution.py:153
  127.2 6.1 %collective-permute-done.14.x = f32[2304,256]{1,0:T(8,128)S(1)} collective-permute-done((f32[2304,256]{1,0:T(8,128)S(1)}, f32[2304,256]{1,0:T(8,128)S(1)}, u32[]{:S(2)}, u32[]{:S(2)}) %collective-permute-start.14) | collective-permute-done | bytes 2359328 | tf_op jit(solution)/shard_map/ppermute | solution.py:569
  136.1 6.5 %collective-permute-done.16.p1 = f32[1152,256]{1,0:T(8,128)S(1)} collective-permute-done((f32[1152,256]{1,0:T(8,128)S(1)}, f32[1152,256]{1,0:T(8,128)S(1)}, u32[]{:S(2)}, u32[]{:S(2)}) %collective-permute-start.16) | collective-permute-done | bytes 1179680 | tf_op jit(solution)/shard_map/ppermute | solution.py:569
  143.0 15.9 %collective-permute-done.12.came2.rhs3 = f32[1024,256]{1,0:T(8,128)S(1)} collective-permute-done((f32[1024,256]{1,0:T(8,128)S(1)}, f32[1024,256]{1,0:T(8,128)S(1)}, u32[]{:S(2)}, u32[]{:S(2)}) %collective-permute-start.12) | collective-permute-done | bytes 1048608 | tf_op jit(solution)/shard_map/ppermute | solution.py:569
  159.0 3.9 %shard_map.61 = (f32[1024,256]{1,0:T(8,128)S(1)}, f32[1024,256]{1,0:T(8,128)S(1)}) custom-call(f32[1024,256]{1,0:T(8,128)S(1)} %collective-permute-done.12.came2.rhs3, f32[1024,256]{1,0:T(8,128)S(1)} %collective-permute-done.13.came3.rhs2, f32[1024,256]{1,0:T(8,128)S(1)} %collective-permute-done.13.came3.rhs2, ...), custom_call_target="tpu_custom_call" | custom-call | flops 2415919104 | bytes 4194304 | tf_op jit(solution)/shard_map/pallas_call | solution.py:153
  163.6 3.9 %shard_map.62 = (f32[1024,256]{1,0:T(8,128)S(1)}, f32[1024,256]{1,0:T(8,128)S(1)}) custom-call(f32[1024,256]{1,0:T(8,128)S(1)} %collective-permute-done.19.came2.came3, f32[1024,256]{1,0:T(8,128)S(1)} %collective-permute-done.19.came2.came3, f32[1024,256]{1,0:T(8,128)S(1)} %collective-permute-done.13.came3.rhs2, ...), custom_call_target="tpu_custom_call" | custom-call | flops 2415919104 | bytes 4194304 | tf_op jit(solution)/shard_map/pallas_call | solution.py:153
  169.8 38.2 %collective-permute-done.21.came = f32[1024,256]{1,0:T(8,128)S(1)} collective-permute-done((f32[1024,256]{1,0:T(8,128)S(1)}, f32[1024,256]{1,0:T(8,128)S(1)}, u32[]{:S(2)}, u32[]{:S(2)}) %collective-permute-start.21) | collective-permute-done | bytes 1048608 | tf_op jit(solution)/shard_map/ppermute | solution.py:569
  208.0 8.3 %shard_map.64 = (f32[1024,256]{1,0:T(8,128)S(1)}, f32[1024,256]{1,0:T(8,128)S(1)}, f32[1024,256]{1,0:T(8,128)S(1)}) custom-call(f32[1024,256]{1,0:T(8,128)S(1)} %bitcast.17, f32[1024,256]{1,0:T(8,128)S(1)} %collective-permute-done.5.ends.ends_in, f32[1024,256]{1,0:T(8,128)S(1)} %collective-permute-done.20.even_in, f32[1024,256]{1,0:T(8,128)S(1)} %get-tuple-element.23.ca1, ...), custom_call_target="tpu_custom_call" | custom-call | flops 3623878656 | bytes 4194304 | tf_op jit(solution)/shard_map/pallas_call | solution.py:153
  220.3 4.0 %collective-permute-done.24.b = f32[8,256]{1,0:T(8,128)S(1)} collective-permute-done((f32[8,256]{1,0:T(8,128)S(1)}, f32[8,256]{1,0:T(8,128)S(1)}, u32[]{:S(2)}, u32[]{:S(2)}) %collective-permute-start.24) | collective-permute-done | bytes 8224 | tf_op jit(solution)/shard_map/ppermute | solution.py:569
  226.9 6.7 %shard_map.66 = f32[4,1024,256]{2,1,0:T(8,128)} custom-call(f32[1024,256]{1,0:T(8,128)S(1)} %collective-permute-done.22.x0, f32[1024,256]{1,0:T(8,128)S(1)} %get-tuple-element.27.x.xa, f32[1024,256]{1,0:T(8,128)S(1)} %shard_map.65.xb, f32[1024,256]{1,0:T(8,128)S(1)} %get-tuple-element.28.coarse, bf16[4,2304,256]{2,1,0:T(8,128)(2,1)S(1)} %bitcast.13, ...), custom_call_target="tpu_custom_call" | custom-call | flops 3623878656 | bytes 4194304 | tf_op jit(solution)/shard_map/pallas_call | solution.py:153
  (53 shorter events, 31.3 us)
Async XLA Ops:
  0.6 4.9 %collective-permute-start = (f32[1024,256]{1,0:T(8,128)}, f32[1024,256]{1,0:T(8,128)S(1)}, u32[]{:S(2)}, u32[]{:S(2)}) collective-permute-start(f32[1024,256]{1,0:T(8,128)} %bitcast.19), channel_id=1, source_target_pairs={{0,4},{4,8},{8,12},{12,16},{16,20},{20,24},{24,28},{28,32},{32,36}... | collective-permute-start | bytes 3145736 | tf_op jit(solution)/shard_map/ppermute | solution.py:569
  16.6 19.2 %collective-permute-start.1 = (f32[1024,256]{1,0:T(8,128)S(1)}, f32[1024,256]{1,0:T(8,128)S(1)}, u32[]{:S(2)}, u32[]{:S(2)}) collective-permute-start(f32[1024,256]{1,0:T(8,128)S(1)} %shard_map.50.relaxed), channel_id=1, source_target_pairs={{0,4},{4,8},{8,12},{12,16},{16,20},{20,24},{24,28},{28,32},{32,36}... | collective-permute-start | bytes 3145736 | tf_op jit(solution)/shard_map/ppermute | solution.py:569
  18.6 45.6 %collective-permute-start.7 = (f32[2304,256]{1,0:T(8,128)S(1)}, f32[2304,256]{1,0:T(8,128)S(1)}, u32[]{:S(2)}, u32[]{:S(2)}) collective-permute-start(f32[2304,256]{1,0:T(8,128)S(1)} %shard_map.53.own), channel_id=1, source_target_pairs={{12,4},{28,20},{44,36},{60,52},{76,68},{92,84},{108,100},{124,116}... | collective-permute-start | bytes 7077896 | tf_op jit(solution)/shard_map/ppermute | solution.py:569
  34.5 33.6 %collective-permute-start.4 = (f32[2304,256]{1,0:T(8,128)S(1)}, f32[2304,256]{1,0:T(8,128)S(1)}, u32[]{:S(2)}, u32[]{:S(2)}) collective-permute-start(f32[2304,256]{1,0:T(8,128)S(1)} %shard_map.53.own), channel_id=1, source_target_pairs={{0,4},{8,12},{16,20},{24,28},{32,36},{40,44},{48,52},{56,60},{64,6... | collective-permute-start | bytes 7077896 | tf_op jit(solution)/shard_map/ppermute | solution.py:569
  43.9 12.6 %collective-permute-start.2 = (f32[1024,256]{1,0:T(8,128)S(1)}, f32[1024,256]{1,0:T(8,128)S(1)}, u32[]{:S(2)}, u32[]{:S(2)}) collective-permute-start(f32[1024,256]{1,0:T(8,128)S(1)} %get-tuple-element.16), channel_id=1, source_target_pairs={{0,4},{8,12},{16,20},{24,28},{32,36},{40,44},{48,52},{56,60},{64,6... | collective-permute-start | bytes 3145736 | tf_op jit(solution)/shard_map/ppermute | solution.py:569
  45.2 34.0 %collective-permute-start.6 = (f32[2304,256]{1,0:T(8,128)S(1)}, f32[2304,256]{1,0:T(8,128)S(1)}, u32[]{:S(2)}, u32[]{:S(2)}) collective-permute-start(f32[2304,256]{1,0:T(8,128)S(1)} %shard_map.53.own), channel_id=1, source_target_pairs={{8,4},{24,20},{40,36},{56,52},{72,68},{88,84},{104,100},{120,116},... | collective-permute-start | bytes 7077896 | tf_op jit(solution)/shard_map/ppermute | solution.py:569
  58.5 15.5 %collective-permute-start.3 = (f32[1024,256]{1,0:T(8,128)S(1)}, f32[1024,256]{1,0:T(8,128)S(1)}, u32[]{:S(2)}, u32[]{:S(2)}) collective-permute-start(f32[1024,256]{1,0:T(8,128)S(1)} %shard_map.52), channel_id=1, source_target_pairs={{4,12},{20,28},{36,44},{52,60},{68,76},{84,92},{100,108},{116,124}... | collective-permute-start | bytes 3145736 | tf_op jit(solution)/shard_map/ppermute | solution.py:569
  59.8 31.8 %collective-permute-start.10 = (f32[1024,256]{1,0:T(8,128)S(1)}, f32[1024,256]{1,0:T(8,128)S(1)}, u32[]{:S(2)}, u32[]{:S(2)}) collective-permute-start(f32[1024,256]{1,0:T(8,128)S(1)} %get-tuple-element.17.rhs.rhs_b.f1.fa1), channel_id=1, source_target_pairs={{12,4},{4,12},{28,20},{20,28},{44,36},{36,44},{60,52},{52,60},{76,... | collective-permute-start | bytes 3145736 | tf_op jit(solution)/shard_map/ppermute | solution.py:569
  64.2 69.2 %collective-permute-start.14 = (f32[2304,256]{1,0:T(8,128)S(1)}, f32[2304,256]{1,0:T(8,128)S(1)}, u32[]{:S(2)}, u32[]{:S(2)}) collective-permute-start(f32[2304,256]{1,0:T(8,128)S(1)} %collective-permute-done.7.x), channel_id=1, source_target_pairs={{60,52},{92,84},{124,116},{61,53},{93,85},{125,117},{62,54},{94,86... | collective-permute-start | bytes 7077896 | tf_op jit(solution)/shard_map/ppermute | solution.py:569
  68.4 40.7 %collective-permute-start.15 = (f32[1152,256]{1,0:T(8,128)S(1)}, f32[1152,256]{1,0:T(8,128)S(1)}, u32[]{:S(2)}, u32[]{:S(2)}) collective-permute-start(f32[1152,256]{1,0:T(8,128)S(1)} %get-tuple-element.19), channel_id=1, source_target_pairs={{4,12},{20,28},{36,44},{52,60},{68,76},{84,92},{100,108},{116,124}... | collective-permute-start | bytes 3538952 | tf_op jit(solution)/shard_map/ppermute | solution.py:569
  74.0 37.5 %collective-permute-start.9 = (f32[1024,256]{1,0:T(8,128)S(1)}, f32[1024,256]{1,0:T(8,128)S(1)}, u32[]{:S(2)}, u32[]{:S(2)}) collective-permute-start(f32[1024,256]{1,0:T(8,128)S(1)} %get-tuple-element.17.rhs.rhs_b.f1.fa1), channel_id=1, source_target_pairs={{8,4},{0,12},{24,20},{16,28},{40,36},{32,44},{56,52},{48,60},{72,6... | collective-permute-start | bytes 3145736 | tf_op jit(solution)/shard_map/ppermute | solution.py:569
  79.2 37.0 %collective-permute-start.8 = (f32[1024,256]{1,0:T(8,128)S(1)}, f32[1024,256]{1,0:T(8,128)S(1)}, u32[]{:S(2)}, u32[]{:S(2)}) collective-permute-start(f32[1024,256]{1,0:T(8,128)S(1)} %get-tuple-element.17.rhs.rhs_b.f1.fa1), channel_id=1, source_target_pairs={{0,4},{16,20},{32,36},{48,52},{64,68},{80,84},{96,100},{112,116},{... | collective-permute-start | bytes 3145736 | tf_op jit(solution)/shard_map/ppermute | solution.py:569
  91.6 26.6 %collective-permute-start.5 = (f32[1024,256]{1,0:T(8,128)S(1)}, f32[1024,256]{1,0:T(8,128)S(1)}, u32[]{:S(2)}, u32[]{:S(2)}) collective-permute-start(f32[1024,256]{1,0:T(8,128)S(1)} %shard_map.55.ends), channel_id=1, source_target_pairs={{12,20},{28,36},{44,52},{60,68},{76,84},{92,100},{108,116},{13,21}... | collective-permute-start | bytes 3145736 | tf_op jit(solution)/shard_map/ppermute | solution.py:569
  109.2 25.5 %collective-permute-start.18 = (f32[1152,256]{1,0:T(8,128)S(1)}, f32[1152,256]{1,0:T(8,128)S(1)}, u32[]{:S(2)}, u32[]{:S(2)}) collective-permute-start(f32[1152,256]{1,0:T(8,128)S(1)} %collective-permute-done.15.p0), channel_id=1, source_target_pairs={{12,15},{13,12},{14,13},{15,14},{28,31},{29,28},{30,29},{31,30},{4... | collective-permute-start | bytes 3538952 | tf_op jit(solution)/shard_map/ppermute | solution.py:569
  111.6 24.5 %collective-permute-start.17 = (f32[1152,256]{1,0:T(8,128)S(1)}, f32[1152,256]{1,0:T(8,128)S(1)}, u32[]{:S(2)}, u32[]{:S(2)}) collective-permute-start(f32[1152,256]{1,0:T(8,128)S(1)} %collective-permute-done.15.p0), channel_id=1, source_target_pairs={{12,14},{13,15},{14,12},{15,13},{28,30},{29,31},{30,28},{31,29},{4... | collective-permute-start | bytes 3538952 | tf_op jit(solution)/shard_map/ppermute | solution.py:569
  116.3 26.4 %collective-permute-start.16 = (f32[1152,256]{1,0:T(8,128)S(1)}, f32[1152,256]{1,0:T(8,128)S(1)}, u32[]{:S(2)}, u32[]{:S(2)}) collective-permute-start(f32[1152,256]{1,0:T(8,128)S(1)} %collective-permute-done.15.p0), channel_id=1, source_target_pairs={{12,13},{13,14},{14,15},{15,12},{28,29},{29,30},{30,31},{31,28},{4... | collective-permute-start | bytes 3538952 | tf_op jit(solution)/shard_map/ppermute | solution.py:569
  126.5 16.6 %collective-permute-start.13 = (f32[1024,256]{1,0:T(8,128)S(1)}, f32[1024,256]{1,0:T(8,128)S(1)}, u32[]{:S(2)}, u32[]{:S(2)}) collective-permute-start(f32[1024,256]{1,0:T(8,128)S(1)} %shard_map.58.own2.made), channel_id=1, source_target_pairs={{20,60},{36,52},{68,84},{100,116},{21,61},{37,53},{69,85},{101,117... | collective-permute-start | bytes 3145736 | tf_op jit(solution)/shard_map/ppermute | solution.py:569
  133.3 25.6 %collective-permute-start.12 = (f32[1024,256]{1,0:T(8,128)S(1)}, f32[1024,256]{1,0:T(8,128)S(1)}, u32[]{:S(2)}, u32[]{:S(2)}) collective-permute-start(f32[1024,256]{1,0:T(8,128)S(1)} %shard_map.58.own2.made), channel_id=1, source_target_pairs={{20,52},{36,60},{68,92},{100,124},{21,53},{37,61},{69,93},{101,125... | collective-permute-start | bytes 3145736 | tf_op jit(solution)/shard_map/ppermute | solution.py:569
  134.6 24.3 %collective-permute-start.11 = (f32[1024,256]{1,0:T(8,128)S(1)}, f32[1024,256]{1,0:T(8,128)S(1)}, u32[]{:S(2)}, u32[]{:S(2)}) collective-permute-start(f32[1024,256]{1,0:T(8,128)S(1)} %shard_map.58.own2.made), channel_id=1, source_target_pairs={{4,12},{20,28},{36,44},{52,60},{68,76},{84,92},{100,108},{116,124}... | collective-permute-start | bytes 3145736 | tf_op jit(solution)/shard_map/ppermute | solution.py:569
  167.7 2.0 collective-permute-start.20
  168.5 39.5 %collective-permute-start.21 = (f32[1024,256]{1,0:T(8,128)S(1)}, f32[1024,256]{1,0:T(8,128)S(1)}, u32[]{:S(2)}, u32[]{:S(2)}) collective-permute-start(f32[1024,256]{1,0:T(8,128)S(1)} %get-tuple-element.22.cb2), channel_id=1, source_target_pairs={{84,116},{92,124},{85,117},{93,125},{86,118},{94,126},{87,119},{95... | collective-permute-start | bytes 3145736 | tf_op jit(solution)/shard_map/ppermute | solution.py:569
  216.3 10.6 %collective-permute-start.22 = (f32[1024,256]{1,0:T(8,128)S(1)}, f32[1024,256]{1,0:T(8,128)S(1)}, u32[]{:S(2)}, u32[]{:S(2)}) collective-permute-start(f32[1024,256]{1,0:T(8,128)S(1)} %get-tuple-element.26), channel_id=1, source_target_pairs={{4,0},{12,8},{20,16},{28,24},{36,32},{44,40},{52,48},{60,56},{68,6... | collective-permute-start | bytes 3145736 | tf_op jit(solution)/shard_map/ppermute | solution.py:569
  217.6 2.6 %collective-permute-start.23 = (f32[8,256]{1,0:T(8,128)S(1)}, f32[8,256]{1,0:T(8,128)S(1)}, u32[]{:S(2)}, u32[]{:S(2)}) collective-permute-start(f32[8,256]{1,0:T(8,128)S(1)} %get-tuple-element.29.a), channel_id=1, source_target_pairs={{0,1},{1,0},{2,3},{3,2},{4,5},{5,4},{6,7},{7,6},{8,9},{9,8},{10,11... | collective-permute-start | bytes 24584 | tf_op jit(solution)/shard_map/ppermute | solution.py:569
  220.2 4.0 %collective-permute-start.24 = (f32[8,256]{1,0:T(8,128)S(1)}, f32[8,256]{1,0:T(8,128)S(1)}, u32[]{:S(2)}, u32[]{:S(2)}) collective-permute-start(f32[8,256]{1,0:T(8,128)S(1)} %shard_map.67.a), channel_id=1, source_target_pairs={{0,2},{2,0},{1,3},{3,1},{4,6},{6,4},{5,7},{7,5},{8,10},{10,8},{9,1... | collective-permute-start | bytes 24584 | tf_op jit(solution)/shard_map/ppermute | solution.py:569
  (5 other events, 42.9 us)
where the time goes:
time: 234 us
  waiting for transfers between devices  119 us (51%)
  Pallas kernels  56.7 us (24%)
  starting transfers between devices  52.7 us (23%)
  local copies, waits for them, and re-layouts  3.57 us (2%)
    ppermute x25, waiting for transfers between devices, send(): return lax.ppermute(value, axis, pairs)  119 us
    pallas_call x19, Pallas kernels, kernel_call(): pl.pallas_call(body, out_shape=outs, in_specs=in_specs, out_specs=out_spe...  56.7 us
    ppermute x25, starting transfers between devices, send(): return lax.ppermute(value, axis, pairs)  52.7 us
  transfers between devices with their start and end apart: 25, of which 12 were waited for; matrix products, arithmetic and copies ran while one was open for 0% of the time, Pallas kernels for 11%

commit v1 on v0

--- a/solution.py
+++ b/solution.py
@@ -345,8 +345,8 @@
     return kernel_call(choose_body, STATE, VMEM, args, [ANY] * 5, [pltpu.SemaphoreType.DMA], 0, 8)
 
 
-def correct_body(first, ends_in, even_in, ca1, ca2, came, rhs2, rhs3, we2, we3, wa0, wb0, wa1, wb1,
-                 fa0, fb0, fa1, fb1, made, got, ends, send, move, coarse, b0, b1, held, xv, xs, wv, ws):
+def correct_body(first, ends_in, even_in, even2_in, ca1, ca2, came, rhs2, rhs3, we2, we3, wa0, wb0, wa1, wb1,
+                 fa0, fb0, fa1, fb1, made, got3, got1, ends, send, move, coarse, b0, b1, held, xv, xs, wv, ws):
     d, xc, z, _ = spot()
     is_a = z % 2 == 0
     is_b = z % 2 == 1
@@ -357,7 +357,7 @@
     x, ra, g0, g1, rk = (xv.at[n] for n in range(5))
     got_x = Load(
         [((xc == 0) & (z < 2), first), ((xc == 0) & (z == 2), ends_in),
-         (((xc == 0) & third) | ((xc > 0) & (z < 2)), even_in),
+         (((xc == 0) & third) | ((xc > 0) & (z < 2) & (d != 25)), even_in), (d == 25, even2_in),
          ((xc == 1) & odd, ca1), ((xc == 2) & odd, ca2), (late, came)], x, xs.at[0])
     got_e = Load([(third, we3), (other, we2)], wv.at[0], ws.at[0])
     got_ra = Load([(third, rhs3), (other, rhs2)], ra, xs.at[1])
@@ -365,7 +365,9 @@
     got_w1 = Load([(is_a, wa1.at[0]), (is_b, wb1)], wv.at[2], ws.at[2])
     got_f0 = Load([(is_a, fa0), (is_b, fb0)], g0, xs.at[2])
     got_f1 = Load([(is_a, fa1), (is_b, fb1)], g1, xs.at[3])
-    got_r = Load([(is_a, made), (is_b & (d // 4 > 0), got), (is_b & (d // 4 == 0), ends)], rk, xs.at[4])
+    got_r = Load(
+        [(is_a, made), (third, got3), ((z == 1) & (d // 4 > 0), got1), ((z == 1) & (d // 4 == 0), ends)],
+        rk, xs.at[4])
     start_all(got_x, got_e, got_ra)
     stencil_pads(b0, b1)
     got_x.wait()
@@ -386,24 +388,23 @@
         value = v + 4 * H * a + g0[r : r + TILE, :]
         move[r : r + TILE, :] = value
         send[r : r + TILE, :] = v
-        return value
-
-    def one(r, v, a):
-        @pl.when(is_b)
-        def _():
-            value = v + 4 * H * a + g1[r : r + TILE, :]
-            move[r : r + TILE, :] = value
-            send[r : r + TILE, :] = value
-
-    run_steps(
-        rows(x), (b0, b1), held,
-        [(ready([got_w0, got_f0, got_r]), wv.at[1], zero), (ready([got_w1, got_f1]), wv.at[2], one)],
-    )
+        stencil_put(b1, r, value)
+
+    run_steps(rows(x), (b0, b1), held, [(ready([got_w0, got_f0, got_r]), wv.at[1], zero)])
+    wait_all(got_w1, got_f1)
+
+    @pl.when(is_b)
+    def _():
+        for r in range(0, ROWS, TILE):
+            at = slice(r, r + TILE)
+            value = move[at, :] + 4 * H * relu_conv(b1, wv.at[2], r) + g1[at, :]
+            move[at, :] = value
+            send[at, :] = value
 
 
 def correct(*args):
     return kernel_call(
-        correct_body, (STATE,) * 3, (VMEM,) * 3, args, [ANY] * 12 + [HBM] + [ANY] * 8,
+        correct_body, (STATE,) * 3, (VMEM,) * 3, args, [ANY] * 13 + [HBM] + [ANY] * 9,
         [*SCRATCH, *room(5), *wbuf(3)], 3, 22
     )
 
@@ -607,14 +608,14 @@
     w_even2 = send(w_z3, [(8 * x + 7, 8 * x + 5) for x in range(1, 4)])
     made = group(first, ends_in, wn_chip, w, wn_z2, wn_z3, fine_a0, fine, fine_2, fine_3)
 
+    in_c = send(made, [(9, 13), (17, 21), (25, 29), (5, 7), (13, 15), (21, 23), (29, 31)])
     in_a = send(made, [(5, 13), (9, 15), (17, 23), (25, 31)])
-    in_b = send(made, [(5, 15), (9, 13), (17, 21), (25, 29)])
-    got = send(made, [(k + 1, k + 3) for k in A0])
+    in_d = send(made, [(5, 15), (1, 3), (9, 11), (17, 19), (25, 27)])
     wn_even2 = narrow(w_even2)
     wn_b0, wn_b1 = unpack(*parts)
 
-    common = (in_b, in_a, wn_even2, wn_z3, wn_chip, wn_b0, made, got)
-    ca1, cb1 = relay(in_a, in_b, *common)
+    common = (in_c, in_a, wn_even2, wn_z3, wn_chip, wn_b0, made, in_c)
+    ca1, cb1 = relay(in_a, in_d, *common)
     came = send(cb1, [(13, 21), (15, 23)])
     swapped = send(squares, [(0, 1), (1, 0), (2, 3), (3, 2)], "batch")
     squares = norm_sum(squares, swapped)
@@ -622,11 +623,12 @@
     norms = norm_root(squares, swapped)
     ca2, cb2 = relay(came, came, *common)
     came = send(cb2, [(21, 29), (23, 31)])
-    carry = choose(ends, made, got, cb1, cb2)
-    even_in = send(carry, [(3, 7), (5, 11), (7, 9), (13, 19), (15, 17), (21, 27), (23, 25)])
+    carry = choose(ends, made, in_c, cb1, cb2)
+    even_in = send(carry, [(3, 7), (5, 11), (7, 9), (13, 19), (15, 17), (21, 27)])
+    even2_in = send(came, [(29, 25)])
     out1, move, coarse = correct(
-        first, ends_in, even_in, ca1, ca2, came, in_b, in_a, wn_even2, wn_z3, wn_chip, wn_b0, w, wn_b1,
-        fine_a0, fine_2, fine, fine_3, made, got, ends,
+        first, ends_in, even_in, even2_in, ca1, ca2, came, in_c, in_a, wn_even2, wn_z3, wn_chip, wn_b0, w, wn_b1,
+        fine_a0, fine_2, fine, fine_3, made, in_c, in_d, ends,
     )
     in1 = send(out1, [p for k in A0 for p in ((k + 1, k), (k + 3, k + 2))])
     moved = second(move, wn_chip, in0)

time: 234 us -> 234 us (level)
  the two profiles are of different devices: /device:TPU:119 before, /device:TPU:7 now
where the time goes in v1:
time: 234 us; the launch traced here: 233 us
  waiting for transfers between devices  120 us (51%)
  starting transfers between devices  58.6 us (25%)
  Pallas kernels  50 us (21%)
  local copies, waits for them, and re-layouts  3.57 us (2%)
    ppermute x26, waiting for transfers between devices, send(): return lax.ppermute(value, axis, pairs)  120 us
    ppermute x26, starting transfers between devices, send(): return lax.ppermute(value, axis, pairs)  58.6 us
    pallas_call x19, Pallas kernels, kernel_call(): pl.pallas_call(body, out_shape=outs, in_specs=in_specs, out_specs=out_spe...  50 us
  transfers between devices with their start and end apart: 26, of which 13 were waited for; matrix products, arithmetic and copies ran while one was open for 0% of the time, Pallas kernels for 10%

profile of v1, /device:TPU:7, one launch (start us, length us, event | category | flops | bytes accessed | tf_op | source)
XLA Modules:
  0.0 233.5 jit_solution(3485248861242269398)
XLA Ops:
  0.6 4.1 %collective-permute-start = (f32[1024,256]{1,0:T(8,128)}, f32[1024,256]{1,0:T(8,128)S(1)}, u32[]{:S(2)}, u32[]{:S(2)}) collective-permute-start(f32[1024,256]{1,0:T(8,128)} %bitcast.19), channel_id=1, source_target_pairs={{0,4},{4,8},{8,12},{12,16},{16,20},{20,24},{24,28},{28,32},{32,36}... | collective-permute-start | bytes 3145736 | tf_op jit(solution)/shard_map/ppermute | solution.py:570
  4.7 12.0 %collective-permute-done.given = f32[1024,256]{1,0:T(8,128)S(1)} collective-permute-done((f32[1024,256]{1,0:T(8,128)}, f32[1024,256]{1,0:T(8,128)S(1)}, u32[]{:S(2)}, u32[]{:S(2)}) %collective-permute-start) | collective-permute-done | bytes 1048608 | tf_op jit(solution)/shard_map/ppermute | solution.py:570
  16.8 2.3 copy-done
  20.3 7.4 %shard_map.50.relaxed = f32[1024,256]{1,0:T(8,128)S(1)} custom-call(f32[1024,256]{1,0:T(8,128)S(1)} %bitcast.14, f32[1024,256]{1,0:T(8,128)S(1)} %collective-permute-done.given, bf16[4,2304,256]{2,1,0:T(8,128)(2,1)S(1)} %bitcast.6), custom_call_target="tpu_custom_call" | custom-call | flops 4831838208 | bytes 4194304 | tf_op jit(solution)/shard_map/pallas_call | solution.py:153
  27.8 4.5 %collective-permute-start.1 = (f32[1024,256]{1,0:T(8,128)S(1)}, f32[1024,256]{1,0:T(8,128)S(1)}, u32[]{:S(2)}, u32[]{:S(2)}) collective-permute-start(f32[1024,256]{1,0:T(8,128)S(1)} %shard_map.50.relaxed), channel_id=1, source_target_pairs={{0,4},{4,8},{8,12},{12,16},{16,20},{20,24},{24,28},{28,32},{32,36}... | collective-permute-start | bytes 3145736 | tf_op jit(solution)/shard_map/ppermute | solution.py:570
  35.4 8.7 %collective-permute-done.1.given = f32[1024,256]{1,0:T(8,128)S(1)} collective-permute-done((f32[1024,256]{1,0:T(8,128)S(1)}, f32[1024,256]{1,0:T(8,128)S(1)}, u32[]{:S(2)}, u32[]{:S(2)}) %collective-permute-start.1) | collective-permute-done | bytes 1048608 | tf_op jit(solution)/shard_map/ppermute | solution.py:570
  44.1 8.0 %shard_map.51 = (f32[1024,256]{1,0:T(8,128)S(1)}, f32[1024,256]{1,0:T(8,128)S(1)}, f32[8,256]{1,0:T(8,128)S(1)}) custom-call(f32[1024,256]{1,0:T(8,128)S(1)} %bitcast.15, f32[1024,256]{1,0:T(8,128)S(1)} %collective-permute-done.1.given, bf16[4,2304,256]{2,1,0:T(8,128)(2,1)S(1)} %bitcast.8, f32[1024,256]{1,0:T(8,128)S(1)} %shard_map.50.relaxed), custom_call_target="tpu_custom_call" | custom-call | flops 4831838208 | bytes 4194304 | tf_op jit(solution)/shard_map/pallas_call | solution.py:153
  54.7 6.0 %collective-permute-done.2.x.rhs_a.f2 = f32[1024,256]{1,0:T(8,128)S(1)} collective-permute-done((f32[1024,256]{1,0:T(8,128)S(1)}, f32[1024,256]{1,0:T(8,128)S(1)}, u32[]{:S(2)}, u32[]{:S(2)}) %collective-permute-start.2) | collective-permute-done | bytes 1048608 | tf_op jit(solution)/shard_map/ppermute | solution.py:570
  67.2 3.4 %collective-permute-start.15 = (f32[1152,256]{1,0:T(8,128)S(1)}, f32[1152,256]{1,0:T(8,128)S(1)}, u32[]{:S(2)}, u32[]{:S(2)}) collective-permute-start(f32[1152,256]{1,0:T(8,128)S(1)} %get-tuple-element.19), channel_id=1, source_target_pairs={{4,12},{20,28},{36,44},{52,60},{68,76},{84,92},{100,108},{116,124}... | collective-permute-start | bytes 3538952 | tf_op jit(solution)/shard_map/ppermute | solution.py:570
  70.6 5.2 %collective-permute-done.3.x = f32[1024,256]{1,0:T(8,128)S(1)} collective-permute-done((f32[1024,256]{1,0:T(8,128)S(1)}, f32[1024,256]{1,0:T(8,128)S(1)}, u32[]{:S(2)}, u32[]{:S(2)}) %collective-permute-start.3) | collective-permute-done | bytes 1048608 | tf_op jit(solution)/shard_map/ppermute | solution.py:570
  77.0 3.9 %shard_map.55.ends = f32[1024,256]{1,0:T(8,128)S(1)} custom-call(f32[1024,256]{1,0:T(8,128)S(1)} %collective-permute-done.3.x, bf16[2304,256]{1,0:T(8,128)(2,1)S(1)} %get-tuple-element.18.wa.w0.w02.wa0.w2, bf16[4,2304,256]{2,1,0:T(8,128)(2,1)S(1)} %bitcast.10, f32[1024,256]{1,0:T(8,128)S(1)} %collective-permute-done.2.x.rhs_a.f2, ...), custom_call_target="tpu_custom_call" | custom-call | flops 2415919104 | bytes 4194304 | tf_op jit(solution)/shard_map/pallas_call | solution.py:153
  80.9 18.0 %collective-permute-done.6.x = f32[2304,256]{1,0:T(8,128)S(1)} collective-permute-done((f32[2304,256]{1,0:T(8,128)S(1)}, f32[2304,256]{1,0:T(8,128)S(1)}, u32[]{:S(2)}, u32[]{:S(2)}) %collective-permute-start.6) | collective-permute-done | bytes 2359328 | tf_op jit(solution)/shard_map/ppermute | solution.py:570
  101.5 9.4 %collective-permute-done.15.p0 = f32[1152,256]{1,0:T(8,128)S(1)} collective-permute-done((f32[1152,256]{1,0:T(8,128)S(1)}, f32[1152,256]{1,0:T(8,128)S(1)}, u32[]{:S(2)}, u32[]{:S(2)}) %collective-permute-start.15) | collective-permute-done | bytes 1179680 | tf_op jit(solution)/shard_map/ppermute | solution.py:570
  113.6 4.3 %collective-permute-done.5.ends.ends_in = f32[1024,256]{1,0:T(8,128)S(1)} collective-permute-done((f32[1024,256]{1,0:T(8,128)S(1)}, f32[1024,256]{1,0:T(8,128)S(1)}, u32[]{:S(2)}, u32[]{:S(2)}) %collective-permute-start.5) | collective-permute-done | bytes 1048608 | tf_op jit(solution)/shard_map/ppermute | solution.py:570
  117.9 8.2 %shard_map.58.own2.made = f32[1024,256]{1,0:T(8,128)S(1)} custom-call(f32[1024,256]{1,0:T(8,128)S(1)} %bitcast.16, f32[1024,256]{1,0:T(8,128)S(1)} %collective-permute-done.5.ends.ends_in, bf16[2304,256]{1,0:T(8,128)(2,1)S(1)} %get-tuple-element.18.wa.w0.w02.wa0.w2, bf16[4,2304,256]{2,1,0:T(8,128)(2,1)S(1)} %bitcast.11, bf16[2304,256]{1,0:T(8,128)(2,1)S(1)} %shard_map.56.w2, ...), custom_call_target="tpu_custom_call" | custom-call | flops 4831838208 | bytes 4194304 | tf_op jit(solution)/shard_map/pallas_call | solution.py:153
  126.1 10.9 %collective-permute-start.13 = (f32[1024,256]{1,0:T(8,128)S(1)}, f32[1024,256]{1,0:T(8,128)S(1)}, u32[]{:S(2)}, u32[]{:S(2)}) collective-permute-start(f32[1024,256]{1,0:T(8,128)S(1)} %shard_map.58.own2.made), channel_id=1, source_target_pairs={{20,60},{4,12},{36,44},{68,76},{100,108},{21,61},{5,13},{37,45},{6... | collective-permute-start | bytes 3145736 | tf_op jit(solution)/shard_map/ppermute | solution.py:570
  139.1 9.0 %collective-permute-start.11 = (f32[1024,256]{1,0:T(8,128)S(1)}, f32[1024,256]{1,0:T(8,128)S(1)}, u32[]{:S(2)}, u32[]{:S(2)}) collective-permute-start(f32[1024,256]{1,0:T(8,128)S(1)} %shard_map.58.own2.made), channel_id=1, source_target_pairs={{36,52},{68,84},{100,116},{20,28},{52,60},{84,92},{116,124},{37,53... | collective-permute-start | bytes 3145736 | tf_op jit(solution)/shard_map/ppermute | solution.py:570
  150.7 9.2 %collective-permute-done.11.rhs2.own3.got.got3 = f32[1024,256]{1,0:T(8,128)S(1)} collective-permute-done((f32[1024,256]{1,0:T(8,128)S(1)}, f32[1024,256]{1,0:T(8,128)S(1)}, u32[]{:S(2)}, u32[]{:S(2)}) %collective-permute-start.11) | collective-permute-done | bytes 1048608 | tf_op jit(solution)/shard_map/ppermute | solution.py:570
  159.9 3.9 %shard_map.61 = (f32[1024,256]{1,0:T(8,128)S(1)}, f32[1024,256]{1,0:T(8,128)S(1)}) custom-call(f32[1024,256]{1,0:T(8,128)S(1)} %collective-permute-done.12.came2.rhs3, f32[1024,256]{1,0:T(8,128)S(1)} %collective-permute-done.13.came3.got1, f32[1024,256]{1,0:T(8,128)S(1)} %collective-permute-done.11.rhs2.own3.got.got3, ...), custom_call_target="tpu_custom_call" | custom-call | flops 2415919104 | bytes 4194304 | tf_op jit(solution)/shard_map/pallas_call | solution.py:153
  164.6 3.9 %shard_map.62 = (f32[1024,256]{1,0:T(8,128)S(1)}, f32[1024,256]{1,0:T(8,128)S(1)}) custom-call(f32[1024,256]{1,0:T(8,128)S(1)} %collective-permute-done.19.came2.came3, f32[1024,256]{1,0:T(8,128)S(1)} %collective-permute-done.19.came2.came3, f32[1024,256]{1,0:T(8,128)S(1)} %collective-permute-done.11.rhs2.own3.got.got3, ...), custom_call_target="tpu_custom_call" | custom-call | flops 2415919104 | bytes 4194304 | tf_op jit(solution)/shard_map/pallas_call | solution.py:153
  171.5 42.9 %collective-permute-done.22.even2_in = f32[1024,256]{1,0:T(8,128)S(1)} collective-permute-done((f32[1024,256]{1,0:T(8,128)S(1)}, f32[1024,256]{1,0:T(8,128)S(1)}, u32[]{:S(2)}, u32[]{:S(2)}) %collective-permute-start.22) | collective-permute-done | bytes 1048608 | tf_op jit(solution)/shard_map/ppermute | solution.py:570
  214.4 3.4 %shard_map.64 = (f32[1024,256]{1,0:T(8,128)S(1)}, f32[1024,256]{1,0:T(8,128)S(1)}, f32[1024,256]{1,0:T(8,128)S(1)}) custom-call(f32[1024,256]{1,0:T(8,128)S(1)} %bitcast.17, f32[1024,256]{1,0:T(8,128)S(1)} %collective-permute-done.5.ends.ends_in, f32[1024,256]{1,0:T(8,128)S(1)} %collective-permute-done.20.even_in, ...), custom_call_target="tpu_custom_call" | custom-call | flops 3623878656 | bytes 4194304 | tf_op jit(solution)/shard_map/pallas_call | solution.py:153
  221.8 2.9 %collective-permute-start.25 = (f32[8,256]{1,0:T(8,128)S(1)}, f32[8,256]{1,0:T(8,128)S(1)}, u32[]{:S(2)}, u32[]{:S(2)}) collective-permute-start(f32[8,256]{1,0:T(8,128)S(1)} %shard_map.67.a), channel_id=1, source_target_pairs={{0,2},{2,0},{1,3},{3,1},{4,6},{6,4},{5,7},{7,5},{8,10},{10,8},{9,1... | collective-permute-start | bytes 24584 | tf_op jit(solution)/shard_map/ppermute | solution.py:570
  226.6 6.7 %shard_map.66 = f32[4,1024,256]{2,1,0:T(8,128)} custom-call(f32[1024,256]{1,0:T(8,128)S(1)} %collective-permute-done.23.x0, f32[1024,256]{1,0:T(8,128)S(1)} %get-tuple-element.27.x.xa, f32[1024,256]{1,0:T(8,128)S(1)} %shard_map.65.xb, f32[1024,256]{1,0:T(8,128)S(1)} %get-tuple-element.28.coarse, bf16[4,2304,256]{2,1,0:T(8,128)(2,1)S(1)} %bitcast.13, ...), custom_call_target="tpu_custom_call" | custom-call | flops 3623878656 | bytes 4194304 | tf_op jit(solution)/shard_map/pallas_call | solution.py:153
  (55 shorter events, 33.8 us)
Async XLA Ops:
  0.6 16.2 %collective-permute-start = (f32[1024,256]{1,0:T(8,128)}, f32[1024,256]{1,0:T(8,128)S(1)}, u32[]{:S(2)}, u32[]{:S(2)}) collective-permute-start(f32[1024,256]{1,0:T(8,128)} %bitcast.19), channel_id=1, source_target_pairs={{0,4},{4,8},{8,12},{12,16},{16,20},{20,24},{24,28},{28,32},{32,36}... | collective-permute-start | bytes 3145736 | tf_op jit(solution)/shard_map/ppermute | solution.py:570
  27.8 16.3 %collective-permute-start.1 = (f32[1024,256]{1,0:T(8,128)S(1)}, f32[1024,256]{1,0:T(8,128)S(1)}, u32[]{:S(2)}, u32[]{:S(2)}) collective-permute-start(f32[1024,256]{1,0:T(8,128)S(1)} %shard_map.50.relaxed), channel_id=1, source_target_pairs={{0,4},{4,8},{8,12},{12,16},{16,20},{20,24},{24,28},{28,32},{32,36}... | collective-permute-start | bytes 3145736 | tf_op jit(solution)/shard_map/ppermute | solution.py:570
  32.8 33.3 %collective-permute-start.7 = (f32[2304,256]{1,0:T(8,128)S(1)}, f32[2304,256]{1,0:T(8,128)S(1)}, u32[]{:S(2)}, u32[]{:S(2)}) collective-permute-start(f32[2304,256]{1,0:T(8,128)S(1)} %shard_map.53.own), channel_id=1, source_target_pairs={{12,4},{28,20},{44,36},{60,52},{76,68},{92,84},{108,100},{124,116}... | collective-permute-start | bytes 7077896 | tf_op jit(solution)/shard_map/ppermute | solution.py:570
  34.1 32.8 %collective-permute-start.4 = (f32[2304,256]{1,0:T(8,128)S(1)}, f32[2304,256]{1,0:T(8,128)S(1)}, u32[]{:S(2)}, u32[]{:S(2)}) collective-permute-start(f32[2304,256]{1,0:T(8,128)S(1)} %shard_map.53.own), channel_id=1, source_target_pairs={{0,4},{8,12},{16,20},{24,28},{32,36},{40,44},{48,52},{56,60},{64,6... | collective-permute-start | bytes 7077896 | tf_op jit(solution)/shard_map/ppermute | solution.py:570
  52.1 8.6 %collective-permute-start.2 = (f32[1024,256]{1,0:T(8,128)S(1)}, f32[1024,256]{1,0:T(8,128)S(1)}, u32[]{:S(2)}, u32[]{:S(2)}) collective-permute-start(f32[1024,256]{1,0:T(8,128)S(1)} %get-tuple-element.16), channel_id=1, source_target_pairs={{0,4},{8,12},{16,20},{24,28},{32,36},{40,44},{48,52},{56,60},{64,6... | collective-permute-start | bytes 3145736 | tf_op jit(solution)/shard_map/ppermute | solution.py:570
  53.4 45.5 %collective-permute-start.6 = (f32[2304,256]{1,0:T(8,128)S(1)}, f32[2304,256]{1,0:T(8,128)S(1)}, u32[]{:S(2)}, u32[]{:S(2)}) collective-permute-start(f32[2304,256]{1,0:T(8,128)S(1)} %shard_map.53.own), channel_id=1, source_target_pairs={{8,4},{24,20},{40,36},{56,52},{72,68},{88,84},{104,100},{120,116},... | collective-permute-start | bytes 7077896 | tf_op jit(solution)/shard_map/ppermute | solution.py:570
  62.7 13.0 %collective-permute-start.3 = (f32[1024,256]{1,0:T(8,128)S(1)}, f32[1024,256]{1,0:T(8,128)S(1)}, u32[]{:S(2)}, u32[]{:S(2)}) collective-permute-start(f32[1024,256]{1,0:T(8,128)S(1)} %shard_map.52), channel_id=1, source_target_pairs={{4,12},{20,28},{36,44},{52,60},{68,76},{84,92},{100,108},{116,124}... | collective-permute-start | bytes 3145736 | tf_op jit(solution)/shard_map/ppermute | solution.py:570
  64.1 36.1 %collective-permute-start.10 = (f32[1024,256]{1,0:T(8,128)S(1)}, f32[1024,256]{1,0:T(8,128)S(1)}, u32[]{:S(2)}, u32[]{:S(2)}) collective-permute-start(f32[1024,256]{1,0:T(8,128)S(1)} %get-tuple-element.17.rhs.rhs_b.f1.fa1), channel_id=1, source_target_pairs={{12,4},{4,12},{28,20},{20,28},{44,36},{36,44},{60,52},{52,60},{76,... | collective-permute-start | bytes 3145736 | tf_op jit(solution)/shard_map/ppermute | solution.py:570
  66.1 70.9 %collective-permute-start.14 = (f32[2304,256]{1,0:T(8,128)S(1)}, f32[2304,256]{1,0:T(8,128)S(1)}, u32[]{:S(2)}, u32[]{:S(2)}) collective-permute-start(f32[2304,256]{1,0:T(8,128)S(1)} %collective-permute-done.7.x), channel_id=1, source_target_pairs={{60,52},{92,84},{124,116},{61,53},{93,85},{125,117},{62,54},{94,86... | collective-permute-start | bytes 7077896 | tf_op jit(solution)/shard_map/ppermute | solution.py:570
  67.2 43.7 %collective-permute-start.15 = (f32[1152,256]{1,0:T(8,128)S(1)}, f32[1152,256]{1,0:T(8,128)S(1)}, u32[]{:S(2)}, u32[]{:S(2)}) collective-permute-start(f32[1152,256]{1,0:T(8,128)S(1)} %get-tuple-element.19), channel_id=1, source_target_pairs={{4,12},{20,28},{36,44},{52,60},{68,76},{84,92},{100,108},{116,124}... | collective-permute-start | bytes 3538952 | tf_op jit(solution)/shard_map/ppermute | solution.py:570
  75.8 36.2 %collective-permute-start.9 = (f32[1024,256]{1,0:T(8,128)S(1)}, f32[1024,256]{1,0:T(8,128)S(1)}, u32[]{:S(2)}, u32[]{:S(2)}) collective-permute-start(f32[1024,256]{1,0:T(8,128)S(1)} %get-tuple-element.17.rhs.rhs_b.f1.fa1), channel_id=1, source_target_pairs={{8,4},{0,12},{24,20},{16,28},{40,36},{32,44},{56,52},{48,60},{72,6... | collective-permute-start | bytes 3145736 | tf_op jit(solution)/shard_map/ppermute | solution.py:570
  98.9 13.9 %collective-permute-start.8 = (f32[1024,256]{1,0:T(8,128)S(1)}, f32[1024,256]{1,0:T(8,128)S(1)}, u32[]{:S(2)}, u32[]{:S(2)}) collective-permute-start(f32[1024,256]{1,0:T(8,128)S(1)} %get-tuple-element.17.rhs.rhs_b.f1.fa1), channel_id=1, source_target_pairs={{0,4},{16,20},{32,36},{48,52},{64,68},{80,84},{96,100},{112,116},{... | collective-permute-start | bytes 3145736 | tf_op jit(solution)/shard_map/ppermute | solution.py:570
  100.2 17.7 %collective-permute-start.5 = (f32[1024,256]{1,0:T(8,128)S(1)}, f32[1024,256]{1,0:T(8,128)S(1)}, u32[]{:S(2)}, u32[]{:S(2)}) collective-permute-start(f32[1024,256]{1,0:T(8,128)S(1)} %shard_map.55.ends), channel_id=1, source_target_pairs={{12,20},{28,36},{44,52},{60,68},{76,84},{92,100},{108,116},{13,21}... | collective-permute-start | bytes 3145736 | tf_op jit(solution)/shard_map/ppermute | solution.py:570
  110.9 28.2 %collective-permute-start.18 = (f32[1152,256]{1,0:T(8,128)S(1)}, f32[1152,256]{1,0:T(8,128)S(1)}, u32[]{:S(2)}, u32[]{:S(2)}) collective-permute-start(f32[1152,256]{1,0:T(8,128)S(1)} %collective-permute-done.15.p0), channel_id=1, source_target_pairs={{12,15},{13,12},{14,13},{15,14},{28,31},{29,28},{30,29},{31,30},{4... | collective-permute-start | bytes 3538952 | tf_op jit(solution)/shard_map/ppermute | solution.py:570
  111.9 36.3 %collective-permute-start.17 = (f32[1152,256]{1,0:T(8,128)S(1)}, f32[1152,256]{1,0:T(8,128)S(1)}, u32[]{:S(2)}, u32[]{:S(2)}) collective-permute-start(f32[1152,256]{1,0:T(8,128)S(1)} %collective-permute-done.15.p0), channel_id=1, source_target_pairs={{12,14},{13,15},{14,12},{15,13},{28,30},{29,31},{30,28},{31,29},{4... | collective-permute-start | bytes 3538952 | tf_op jit(solution)/shard_map/ppermute | solution.py:570
  112.9 35.4 %collective-permute-start.16 = (f32[1152,256]{1,0:T(8,128)S(1)}, f32[1152,256]{1,0:T(8,128)S(1)}, u32[]{:S(2)}, u32[]{:S(2)}) collective-permute-start(f32[1152,256]{1,0:T(8,128)S(1)} %collective-permute-done.15.p0), channel_id=1, source_target_pairs={{12,13},{13,14},{14,15},{15,12},{28,29},{29,30},{30,31},{31,28},{4... | collective-permute-start | bytes 3538952 | tf_op jit(solution)/shard_map/ppermute | solution.py:570
  126.1 22.6 %collective-permute-start.13 = (f32[1024,256]{1,0:T(8,128)S(1)}, f32[1024,256]{1,0:T(8,128)S(1)}, u32[]{:S(2)}, u32[]{:S(2)}) collective-permute-start(f32[1024,256]{1,0:T(8,128)S(1)} %shard_map.58.own2.made), channel_id=1, source_target_pairs={{20,60},{4,12},{36,44},{68,76},{100,108},{21,61},{5,13},{37,45},{6... | collective-permute-start | bytes 3145736 | tf_op jit(solution)/shard_map/ppermute | solution.py:570
  137.0 13.7 %collective-permute-start.12 = (f32[1024,256]{1,0:T(8,128)S(1)}, f32[1024,256]{1,0:T(8,128)S(1)}, u32[]{:S(2)}, u32[]{:S(2)}) collective-permute-start(f32[1024,256]{1,0:T(8,128)S(1)} %shard_map.58.own2.made), channel_id=1, source_target_pairs={{20,52},{36,60},{68,92},{100,124},{21,53},{37,61},{69,93},{101,125... | collective-permute-start | bytes 3145736 | tf_op jit(solution)/shard_map/ppermute | solution.py:570
  139.1 20.9 %collective-permute-start.11 = (f32[1024,256]{1,0:T(8,128)S(1)}, f32[1024,256]{1,0:T(8,128)S(1)}, u32[]{:S(2)}, u32[]{:S(2)}) collective-permute-start(f32[1024,256]{1,0:T(8,128)S(1)} %shard_map.58.own2.made), channel_id=1, source_target_pairs={{36,52},{68,84},{100,116},{20,28},{52,60},{84,92},{116,124},{37,53... | collective-permute-start | bytes 3145736 | tf_op jit(solution)/shard_map/ppermute | solution.py:570
  169.4 2.0 collective-permute-start.20
  170.2 44.2 %collective-permute-start.22 = (f32[1024,256]{1,0:T(8,128)S(1)}, f32[1024,256]{1,0:T(8,128)S(1)}, u32[]{:S(2)}, u32[]{:S(2)}) collective-permute-start(f32[1024,256]{1,0:T(8,128)S(1)} %collective-permute-done.21.came), channel_id=1, source_target_pairs={{116,100},{117,101},{118,102},{119,103}} | collective-permute-start | bytes 3145736 | tf_op jit(solution)/shard_map/ppermute | solution.py:570
  217.9 8.7 %collective-permute-start.23 = (f32[1024,256]{1,0:T(8,128)S(1)}, f32[1024,256]{1,0:T(8,128)S(1)}, u32[]{:S(2)}, u32[]{:S(2)}) collective-permute-start(f32[1024,256]{1,0:T(8,128)S(1)} %get-tuple-element.26), channel_id=1, source_target_pairs={{4,0},{12,8},{20,16},{28,24},{36,32},{44,40},{52,48},{60,56},{68,6... | collective-permute-start | bytes 3145736 | tf_op jit(solution)/shard_map/ppermute | solution.py:570
  219.2 2.6 %collective-permute-start.24 = (f32[8,256]{1,0:T(8,128)S(1)}, f32[8,256]{1,0:T(8,128)S(1)}, u32[]{:S(2)}, u32[]{:S(2)}) collective-permute-start(f32[8,256]{1,0:T(8,128)S(1)} %get-tuple-element.29.a), channel_id=1, source_target_pairs={{0,1},{1,0},{2,3},{3,2},{4,5},{5,4},{6,7},{7,6},{8,9},{9,8},{10,11... | collective-permute-start | bytes 24584 | tf_op jit(solution)/shard_map/ppermute | solution.py:570
  221.8 4.0 %collective-permute-start.25 = (f32[8,256]{1,0:T(8,128)S(1)}, f32[8,256]{1,0:T(8,128)S(1)}, u32[]{:S(2)}, u32[]{:S(2)}) collective-permute-start(f32[8,256]{1,0:T(8,128)S(1)} %shard_map.67.a), channel_id=1, source_target_pairs={{0,2},{2,0},{1,3},{3,1},{4,6},{6,4},{5,7},{7,5},{8,10},{10,8},{9,1... | collective-permute-start | bytes 24584 | tf_op jit(solution)/shard_map/ppermute | solution.py:570
  (6 other events, 38.5 us)

commit v2 on v1

--- a/solution.py
+++ b/solution.py
@@ -5,6 +5,9 @@
 from jax.experimental.pallas import tpu as pltpu
 from jax.sharding import PartitionSpec as P
 
+
+(WIDEN, PACK, SWEEP, RESWEEP, ONE, TWO, NARROW_2, NARROW_3, GROUP, UNPACK, NARROW_E, RELAY1, NORM_SUM, NORM_ROOT, RELAY2,
+ CHOOSE, CORRECT, SECOND, FINISH) = range(100, 119)
 
 CH = 256
 SIDE = 32
@@ -149,9 +152,25 @@
     return None
 
 
-def kernel_call(body, outs, out_specs, args, in_specs, scratch, convs, grant, aliases=None):
+def roles():
+    _, _, z, core = spot()
+    one = core == 1
+    return {ONE: one & (z % 2 == 0), TWO: one & (z % 2 == 1), GROUP: one & (z % 2 == 0), RELAY1: one & (z >= 2),
+            RELAY2: one & (z >= 2), CORRECT: one}
+
+
+def guarded(body, name):
+    def run(*refs):
+        @pl.when(roles()[name])
+        def _():
+            body(*refs)
+
+    return run if name in (ONE, TWO, GROUP, RELAY1, RELAY2, CORRECT) else body
+
+
+def kernel_call(body, outs, out_specs, args, in_specs, scratch, convs, name, grant, aliases=None):
     return pl.pallas_call(
-        body,
+        guarded(body, name),
         out_shape=outs,
         in_specs=in_specs,
         out_specs=out_specs,
@@ -182,7 +201,9 @@
 
 
 def sweep(first, given, w):
-    return kernel_call(sweep_body, STATE, VMEM, (first, given, w), [VMEM, VMEM, HBM], [*SCRATCH[:2], *wbuf(4)], 4, 16)
+    return kernel_call(
+        sweep_body, STATE, VMEM, (first, given, w), [VMEM, VMEM, HBM], [*SCRATCH[:2], *wbuf(4)], 4, SWEEP, 16
+    )
 
 
 def resweep_body(first, given, w, relaxed, fine, send, squares, b0, b1, held, ahead, sums, wv, ws):
@@ -218,7 +239,7 @@
         resweep_body, (STATE, STATE, jax.ShapeDtypeStruct((8, CH), jnp.float32)), (VMEM,) * 3,
         (first, given, w, relaxed), [VMEM, VMEM, HBM, VMEM],
         [*SCRATCH, pltpu.VMEM((2, ROWS, CH), jnp.float32), pltpu.VMEM((2, 8, CH), jnp.float32), *wbuf(4)], 4,
-        20,
+        RESWEEP, 20,
     )
 
 
@@ -244,7 +265,7 @@
 def one_coarse(x, w, rhs):
     return kernel_call(
         one_coarse_body, STATE, VMEM, (x, w, rhs), [VMEM, HBM, ANY], [*SCRATCH, *room(1), *wbuf(1)], 1,
-        14,
+        ONE, 14,
     )
 
 
@@ -263,7 +284,7 @@
 def two_coarse(x, wa, w, rhs_a, rhs_b):
     return kernel_call(
         two_coarse_body, STATE, VMEM, (x, wa, w, rhs_a, rhs_b), [VMEM, ANY, HBM, ANY, ANY],
-        [*SCRATCH, *room(2), *wbuf(2)], 2, 16,
+        [*SCRATCH, *room(2), *wbuf(2)], 2, TWO, 16,
     )
 
 
@@ -299,7 +320,7 @@
 def group(*args):
     return kernel_call(
         group_body, STATE, VMEM, args, [VMEM, VMEM, ANY, HBM] + [ANY] * 6,
-        [*SCRATCH, pltpu.VMEM((2, ROWS, CH), jnp.float32), *room(4), *wbuf(4)], 4, 22,
+        [*SCRATCH, pltpu.VMEM((2, ROWS, CH), jnp.float32), *room(4), *wbuf(4)], 4, GROUP, 22,
     )
 
 
@@ -326,10 +347,10 @@
     )
 
 
-def relay(*args):
+def relay(name, *args):
     return kernel_call(
         relay_body, (STATE, STATE), (VMEM, VMEM), args, [VMEM] * 4 + [ANY] * 4 + [VMEM] * 2, [*SCRATCH, *wbuf(2)], 2,
-        16,
+        name, 16,
     )
 
 
@@ -342,7 +363,7 @@
 
 
 def choose(*args):
-    return kernel_call(choose_body, STATE, VMEM, args, [ANY] * 5, [pltpu.SemaphoreType.DMA], 0, 8)
+    return kernel_call(choose_body, STATE, VMEM, args, [ANY] * 5, [pltpu.SemaphoreType.DMA], 0, CHOOSE, 8)
 
 
 def correct_body(first, ends_in, even_in, even2_in, ca1, ca2, came, rhs2, rhs3, we2, we3, wa0, wb0, wa1, wb1,
@@ -405,7 +426,7 @@
 def correct(*args):
     return kernel_call(
         correct_body, (STATE,) * 3, (VMEM,) * 3, args, [ANY] * 13 + [HBM] + [ANY] * 9,
-        [*SCRATCH, *room(5), *wbuf(3)], 3, 22
+        [*SCRATCH, *room(5), *wbuf(3)], 3, CORRECT, 22
     )
 
 
@@ -421,7 +442,9 @@
 
 
 def second(x, w2, f2):
-    return kernel_call(second_body, STATE, VMEM, (x, w2, f2), [VMEM, ANY, VMEM], [*SCRATCH, *wbuf(1)], 1, 12)
+    return kernel_call(
+        second_body, STATE, VMEM, (x, w2, f2), [VMEM, ANY, VMEM], [*SCRATCH, *wbuf(1)], 1, SECOND, 12
+    )
 
 
 def finish_body(x0, xa, xb, coarse, w, rhs, out, b0, b1, held, wv, ws, stage, os):
@@ -470,7 +493,7 @@
 def finish(*args):
     return kernel_call(
         finish_body, OUT, ANY, args, [VMEM] * 4 + [HBM, VMEM],
-        [*SCRATCH, *wbuf(3), pltpu.VMEM((4, ROWS, CH), jnp.float32), pltpu.SemaphoreType.DMA((4,))], 3, 22,
+        [*SCRATCH, *wbuf(3), pltpu.VMEM((4, ROWS, CH), jnp.float32), pltpu.SemaphoreType.DMA((4,))], 3, FINISH, 22,
     )
 
 
@@ -488,7 +511,7 @@
 def widen(w):
     return kernel_call(
         widen_body, jax.ShapeDtypeStruct((TAPS, CH), jnp.float32), VMEM, (w,), [HBM],
-        [pltpu.VMEM((TAPS, CH), jnp.bfloat16), pltpu.SemaphoreType.DMA], 0, 8,
+        [pltpu.VMEM((TAPS, CH), jnp.bfloat16), pltpu.SemaphoreType.DMA], 0, WIDEN, 8,
     )
 
 
@@ -497,7 +520,9 @@
 
 
 def norm_sum(a, b):
-    return kernel_call(norm_sum_body, jax.ShapeDtypeStruct((8, CH), jnp.float32), VMEM, (a, b), [VMEM, VMEM], [], 0, 2)
+    return kernel_call(
+        norm_sum_body, jax.ShapeDtypeStruct((8, CH), jnp.float32), VMEM, (a, b), [VMEM, VMEM], [], 0, NORM_SUM, 2
+    )
 
 
 def norm_root_body(a, b, out):
@@ -509,7 +534,7 @@
 def norm_root(a, b):
     return kernel_call(
         norm_root_body, jax.ShapeDtypeStruct((1,), jnp.float32), pl.BlockSpec(memory_space=pltpu.SMEM), (a, b),
-        [VMEM, VMEM], [], 0, 2,
+        [VMEM, VMEM], [], 0, NORM_ROOT, 2,
     )
 
 
@@ -520,8 +545,10 @@
         out[at, :] = x[at, :].astype(jnp.bfloat16)
 
 
-def narrow(x):
-    return kernel_call(narrow_body, jax.ShapeDtypeStruct((TAPS, CH), jnp.bfloat16), VMEM, (x,), [VMEM], [], 0, 8)
+def narrow(x, name):
+    return kernel_call(
+        narrow_body, jax.ShapeDtypeStruct((TAPS, CH), jnp.bfloat16), VMEM, (x,), [VMEM], [], 0, name, 8
+    )
 
 
 PART = TAPS // 4
@@ -545,7 +572,7 @@
 def pack(chip, own):
     return kernel_call(
         pack_body, (jax.ShapeDtypeStruct((TAPS, CH), jnp.bfloat16), jax.ShapeDtypeStruct((2 * PART, CH), jnp.float32)),
-        (VMEM, VMEM), (chip, own), [VMEM, VMEM], [], 0, 8,
+        (VMEM, VMEM), (chip, own), [VMEM, VMEM], [], 0, PACK, 8,
     )
 
 
@@ -563,7 +590,7 @@
 
 def unpack(*parts):
     kernel = jax.ShapeDtypeStruct((TAPS, CH), jnp.bfloat16)
-    return kernel_call(unpack_body, (kernel, kernel), (VMEM, VMEM), parts, [VMEM] * 4, [], 0, 10)
+    return kernel_call(unpack_body, (kernel, kernel), (VMEM, VMEM), parts, [VMEM] * 4, [], 0, UNPACK, 10)
 
 
 def send(value, pairs, axis="layer"):
@@ -604,24 +631,24 @@
     for n in (1, 2, 3):
         ring = [((k + 3) * 4 + y, (k + 3) * 4 + (y + n) % 4) for k in A0 for y in range(4)]
         parts.append(send(part0, ring, ("layer", "batch")))
-    wn_z2, wn_z3 = narrow(w_z2), narrow(w_z3)
+    wn_z2, wn_z3 = narrow(w_z2, NARROW_2), narrow(w_z3, NARROW_3)
     w_even2 = send(w_z3, [(8 * x + 7, 8 * x + 5) for x in range(1, 4)])
     made = group(first, ends_in, wn_chip, w, wn_z2, wn_z3, fine_a0, fine, fine_2, fine_3)
 
     in_c = send(made, [(9, 13), (17, 21), (25, 29), (5, 7), (13, 15), (21, 23), (29, 31)])
     in_a = send(made, [(5, 13), (9, 15), (17, 23), (25, 31)])
     in_d = send(made, [(5, 15), (1, 3), (9, 11), (17, 19), (25, 27)])
-    wn_even2 = narrow(w_even2)
+    wn_even2 = narrow(w_even2, NARROW_E)
     wn_b0, wn_b1 = unpack(*parts)
 
     common = (in_c, in_a, wn_even2, wn_z3, wn_chip, wn_b0, made, in_c)
-    ca1, cb1 = relay(in_a, in_d, *common)
+    ca1, cb1 = relay(RELAY1, in_a, in_d, *common)
     came = send(cb1, [(13, 21), (15, 23)])
     swapped = send(squares, [(0, 1), (1, 0), (2, 3), (3, 2)], "batch")
     squares = norm_sum(squares, swapped)
     swapped = send(squares, [(0, 2), (2, 0), (1, 3), (3, 1)], "batch")
     norms = norm_root(squares, swapped)
-    ca2, cb2 = relay(came, came, *common)
+    ca2, cb2 = relay(RELAY2, came, came, *common)
     came = send(cb2, [(21, 29), (23, 31)])
     carry = choose(ends, made, in_c, cb1, cb2)
     even_in = send(carry, [(3, 7), (5, 11), (7, 9), (13, 19), (15, 17), (21, 27)])

time: 234 us -> 234 us (level)
  the two profiles are of different devices: /device:TPU:7 before, /device:TPU:15 now
where the time goes in v2:
time: 234 us; the launch traced here: 233 us
  waiting for transfers between devices  134 us (57%)
  starting transfers between devices  56.7 us (24%)
  Pallas kernels  38.4 us (16%)
  local copies, waits for them, and re-layouts  3.57 us (2%)
    ppermute x26, waiting for transfers between devices, send(): return lax.ppermute(value, axis, pairs)  134 us
    ppermute x26, starting transfers between devices, send(): return lax.ppermute(value, axis, pairs)  56.7 us
    pallas_call x19, Pallas kernels, kernel_call(): pl.pallas_call(guarded(body, name), out_shape=outs, in_specs=in_specs, ou...  38.4 us
  transfers between devices with their start and end apart: 26, of which 13 were waited for; matrix products, arithmetic and copies ran while one was open for 0% of the time, Pallas kernels for 9%

profile of v2, /device:TPU:15, one launch (start us, length us, event | category | flops | bytes accessed | tf_op | source)
XLA Modules:
  0.0 233.4 jit_solution(15487778091239766288)
XLA Ops:
  0.6 4.1 %collective-permute-start = (f32[1024,256]{1,0:T(8,128)}, f32[1024,256]{1,0:T(8,128)S(1)}, u32[]{:S(2)}, u32[]{:S(2)}) collective-permute-start(f32[1024,256]{1,0:T(8,128)} %bitcast.19), channel_id=1, source_target_pairs={{0,4},{4,8},{8,12},{12,16},{16,20},{20,24},{24,28},{28,32},{32,36}... | collective-permute-start | bytes 3145736 | tf_op jit(solution)/shard_map/ppermute | solution.py:597
  4.7 12.0 %collective-permute-done.given = f32[1024,256]{1,0:T(8,128)S(1)} collective-permute-done((f32[1024,256]{1,0:T(8,128)}, f32[1024,256]{1,0:T(8,128)S(1)}, u32[]{:S(2)}, u32[]{:S(2)}) %collective-permute-start) | collective-permute-done | bytes 1048608 | tf_op jit(solution)/shard_map/ppermute | solution.py:597
  16.8 2.3 %copy-done = bf16[4,3,3,256,256]{4,3,2,1,0:T(8,128)(2,1)S(1)} copy-done((bf16[4,3,3,256,256]{4,3,2,1,0:T(8,128)(2,1)S(1)}, bf16[4,3,3,256,256]{4,3,2,1,0:T(8,128)(2,1)}, u32[]{:S(2)}) %copy-start) | copy-done | bytes 4718616
  20.3 7.4 %shard_map.50.relaxed = f32[1024,256]{1,0:T(8,128)S(1)} custom-call(f32[1024,256]{1,0:T(8,128)S(1)} %bitcast.14, f32[1024,256]{1,0:T(8,128)S(1)} %collective-permute-done.given, bf16[4,2304,256]{2,1,0:T(8,128)(2,1)S(1)} %bitcast.6), custom_call_target="tpu_custom_call" | custom-call | flops 4831838208 | bytes 4194304 | tf_op jit(solution)/shard_map/pallas_call | solution.py:172
  27.8 4.5 %collective-permute-start.1 = (f32[1024,256]{1,0:T(8,128)S(1)}, f32[1024,256]{1,0:T(8,128)S(1)}, u32[]{:S(2)}, u32[]{:S(2)}) collective-permute-start(f32[1024,256]{1,0:T(8,128)S(1)} %shard_map.50.relaxed), channel_id=1, source_target_pairs={{0,4},{4,8},{8,12},{12,16},{16,20},{20,24},{24,28},{28,32},{32,36}... | collective-permute-start | bytes 3145736 | tf_op jit(solution)/shard_map/ppermute | solution.py:597
  35.4 8.7 %collective-permute-done.1.given = f32[1024,256]{1,0:T(8,128)S(1)} collective-permute-done((f32[1024,256]{1,0:T(8,128)S(1)}, f32[1024,256]{1,0:T(8,128)S(1)}, u32[]{:S(2)}, u32[]{:S(2)}) %collective-permute-start.1) | collective-permute-done | bytes 1048608 | tf_op jit(solution)/shard_map/ppermute | solution.py:597
  44.1 8.0 %shard_map.51 = (f32[1024,256]{1,0:T(8,128)S(1)}, f32[1024,256]{1,0:T(8,128)S(1)}, f32[8,256]{1,0:T(8,128)S(1)}) custom-call(f32[1024,256]{1,0:T(8,128)S(1)} %bitcast.15, f32[1024,256]{1,0:T(8,128)S(1)} %collective-permute-done.1.given, bf16[4,2304,256]{2,1,0:T(8,128)(2,1)S(1)} %bitcast.8, f32[1024,256]{1,0:T(8,128)S(1)} %shard_map.50.relaxed), custom_call_target="tpu_custom_call" | custom-call | flops 4831838208 | bytes 4194304 | tf_op jit(solution)/shard_map/pallas_call | solution.py:172
  54.7 6.0 %collective-permute-done.2.refs_0_.refs_3_.f2 = f32[1024,256]{1,0:T(8,128)S(1)} collective-permute-done((f32[1024,256]{1,0:T(8,128)S(1)}, f32[1024,256]{1,0:T(8,128)S(1)}, u32[]{:S(2)}, u32[]{:S(2)}) %collective-permute-start.2) | collective-permute-done | bytes 1048608 | tf_op jit(solution)/shard_map/ppermute | solution.py:597
  67.2 3.4 %collective-permute-start.15 = (f32[1152,256]{1,0:T(8,128)S(1)}, f32[1152,256]{1,0:T(8,128)S(1)}, u32[]{:S(2)}, u32[]{:S(2)}) collective-permute-start(f32[1152,256]{1,0:T(8,128)S(1)} %get-tuple-element.19), channel_id=1, source_target_pairs={{4,12},{20,28},{36,44},{52,60},{68,76},{84,92},{100,108},{116,124}... | collective-permute-start | bytes 3538952 | tf_op jit(solution)/shard_map/ppermute | solution.py:597
  70.6 5.2 %collective-permute-done.3.refs_0_ = f32[1024,256]{1,0:T(8,128)S(1)} collective-permute-done((f32[1024,256]{1,0:T(8,128)S(1)}, f32[1024,256]{1,0:T(8,128)S(1)}, u32[]{:S(2)}, u32[]{:S(2)}) %collective-permute-start.3) | collective-permute-done | bytes 1048608 | tf_op jit(solution)/shard_map/ppermute | solution.py:597
  77.1 21.8 %collective-permute-done.6.x = f32[2304,256]{1,0:T(8,128)S(1)} collective-permute-done((f32[2304,256]{1,0:T(8,128)S(1)}, f32[2304,256]{1,0:T(8,128)S(1)}, u32[]{:S(2)}, u32[]{:S(2)}) %collective-permute-start.6) | collective-permute-done | bytes 2359328 | tf_op jit(solution)/shard_map/ppermute | solution.py:597
  101.5 9.4 %collective-permute-done.15.p0 = f32[1152,256]{1,0:T(8,128)S(1)} collective-permute-done((f32[1152,256]{1,0:T(8,128)S(1)}, f32[1152,256]{1,0:T(8,128)S(1)}, u32[]{:S(2)}, u32[]{:S(2)}) %collective-permute-start.15) | collective-permute-done | bytes 1179680 | tf_op jit(solution)/shard_map/ppermute | solution.py:597
  113.6 4.3 %collective-permute-done.5.refs_1_ = f32[1024,256]{1,0:T(8,128)S(1)} collective-permute-done((f32[1024,256]{1,0:T(8,128)S(1)}, f32[1024,256]{1,0:T(8,128)S(1)}, u32[]{:S(2)}, u32[]{:S(2)}) %collective-permute-start.5) | collective-permute-done | bytes 1048608 | tf_op jit(solution)/shard_map/ppermute | solution.py:597
  117.9 8.2 %shard_map.58.refs_8_.made.refs_19_ = f32[1024,256]{1,0:T(8,128)S(1)} custom-call(f32[1024,256]{1,0:T(8,128)S(1)} %bitcast.16, f32[1024,256]{1,0:T(8,128)S(1)} %collective-permute-done.5.refs_1_, bf16[2304,256]{1,0:T(8,128)(2,1)S(1)} %get-tuple-element.18.refs_1_.refs_2_.refs_6_.refs_11_.w2, bf16[4,2304,256]{2,1,0:T(8,128)(2,1)S(1)} %bitcast.11, ...), custom_call_target="tpu_custom_call" | custom-call | flops 4831838208 | bytes 4194304 | tf_op jit(solution)/shard_map/pallas_call | solution.py:172
  126.1 3.0 %collective-permute-start.13 = (f32[1024,256]{1,0:T(8,128)S(1)}, f32[1024,256]{1,0:T(8,128)S(1)}, u32[]{:S(2)}, u32[]{:S(2)}) collective-permute-start(f32[1024,256]{1,0:T(8,128)S(1)} %shard_map.58.refs_8_.made.refs_19_), channel_id=1, source_target_pairs={{20,60},{4,12},{36,44},{68,76},{100,108},{21,61},{5,13},{37,45},{6... | collective-permute-start | bytes 3145736 | tf_op jit(solution)/shard_map/ppermute | solution.py:597
  129.1 10.0 %collective-permute-start.12 = (f32[1024,256]{1,0:T(8,128)S(1)}, f32[1024,256]{1,0:T(8,128)S(1)}, u32[]{:S(2)}, u32[]{:S(2)}) collective-permute-start(f32[1024,256]{1,0:T(8,128)S(1)} %shard_map.58.refs_8_.made.refs_19_), channel_id=1, source_target_pairs={{20,52},{36,60},{68,92},{100,124},{21,53},{37,61},{69,93},{101,125... | collective-permute-start | bytes 3145736 | tf_op jit(solution)/shard_map/ppermute | solution.py:597
  139.1 9.2 %collective-permute-start.11 = (f32[1024,256]{1,0:T(8,128)S(1)}, f32[1024,256]{1,0:T(8,128)S(1)}, u32[]{:S(2)}, u32[]{:S(2)}) collective-permute-start(f32[1024,256]{1,0:T(8,128)S(1)} %shard_map.58.refs_8_.made.refs_19_), channel_id=1, source_target_pairs={{36,52},{68,84},{100,116},{20,28},{52,60},{84,92},{116,124},{37,53... | collective-permute-start | bytes 3145736 | tf_op jit(solution)/shard_map/ppermute | solution.py:597
  150.7 9.2 %collective-permute-done.11.refs_2_.refs_9_.got.refs_7_.refs_20_ = f32[1024,256]{1,0:T(8,128)S(1)} collective-permute-done((f32[1024,256]{1,0:T(8,128)S(1)}, f32[1024,256]{1,0:T(8,128)S(1)}, u32[]{:S(2)}, u32[]{:S(2)}) %collective-permute-start.11) | collective-permute-done | bytes 1048608 | tf_op jit(solution)/shard_map/ppermute | solution.py:597
  163.7 50.7 %collective-permute-done.22.refs_3_ = f32[1024,256]{1,0:T(8,128)S(1)} collective-permute-done((f32[1024,256]{1,0:T(8,128)S(1)}, f32[1024,256]{1,0:T(8,128)S(1)}, u32[]{:S(2)}, u32[]{:S(2)}) %collective-permute-start.22) | collective-permute-done | bytes 1048608 | tf_op jit(solution)/shard_map/ppermute | solution.py:597
  214.4 3.4 %shard_map.64 = (f32[1024,256]{1,0:T(8,128)S(1)}, f32[1024,256]{1,0:T(8,128)S(1)}, f32[1024,256]{1,0:T(8,128)S(1)}) custom-call(f32[1024,256]{1,0:T(8,128)S(1)} %bitcast.17, f32[1024,256]{1,0:T(8,128)S(1)} %collective-permute-done.5.refs_1_, f32[1024,256]{1,0:T(8,128)S(1)} %collective-permute-done.20.refs_2_, ...), custom_call_target="tpu_custom_call" | custom-call | flops 3623878656 | bytes 4194304 | tf_op jit(solution)/shard_map/pallas_call | solution.py:172
  219.4 2.3 %collective-permute-done.24.b = f32[8,256]{1,0:T(8,128)S(1)} collective-permute-done((f32[8,256]{1,0:T(8,128)S(1)}, f32[8,256]{1,0:T(8,128)S(1)}, u32[]{:S(2)}, u32[]{:S(2)}) %collective-permute-start.24) | collective-permute-done | bytes 8224 | tf_op jit(solution)/shard_map/ppermute | solution.py:597
  221.8 2.0 collective-permute-start.25
  223.8 2.0 collective-permute-done.25.b
  226.5 6.7 %shard_map.66 = f32[4,1024,256]{2,1,0:T(8,128)} custom-call(f32[1024,256]{1,0:T(8,128)S(1)} %collective-permute-done.23.x0, f32[1024,256]{1,0:T(8,128)S(1)} %get-tuple-element.27.x.xa, f32[1024,256]{1,0:T(8,128)S(1)} %shard_map.65.xb, f32[1024,256]{1,0:T(8,128)S(1)} %get-tuple-element.28.coarse, bf16[4,2304,256]{2,1,0:T(8,128)(2,1)S(1)} %bitcast.13, ...), custom_call_target="tpu_custom_call" | custom-call | flops 3623878656 | bytes 4194304 | tf_op jit(solution)/shard_map/pallas_call | solution.py:172
  (55 shorter events, 28.2 us)
Async XLA Ops:
  0.6 16.2 %collective-permute-start = (f32[1024,256]{1,0:T(8,128)}, f32[1024,256]{1,0:T(8,128)S(1)}, u32[]{:S(2)}, u32[]{:S(2)}) collective-permute-start(f32[1024,256]{1,0:T(8,128)} %bitcast.19), channel_id=1, source_target_pairs={{0,4},{4,8},{8,12},{12,16},{16,20},{20,24},{24,28},{28,32},{32,36}... | collective-permute-start | bytes 3145736 | tf_op jit(solution)/shard_map/ppermute | solution.py:597
  27.8 16.3 %collective-permute-start.1 = (f32[1024,256]{1,0:T(8,128)S(1)}, f32[1024,256]{1,0:T(8,128)S(1)}, u32[]{:S(2)}, u32[]{:S(2)}) collective-permute-start(f32[1024,256]{1,0:T(8,128)S(1)} %shard_map.50.relaxed), channel_id=1, source_target_pairs={{0,4},{4,8},{8,12},{12,16},{16,20},{20,24},{24,28},{28,32},{32,36}... | collective-permute-start | bytes 3145736 | tf_op jit(solution)/shard_map/ppermute | solution.py:597
  32.8 33.3 %collective-permute-start.7 = (f32[2304,256]{1,0:T(8,128)S(1)}, f32[2304,256]{1,0:T(8,128)S(1)}, u32[]{:S(2)}, u32[]{:S(2)}) collective-permute-start(f32[2304,256]{1,0:T(8,128)S(1)} %shard_map.53.own), channel_id=1, source_target_pairs={{12,4},{28,20},{44,36},{60,52},{76,68},{92,84},{108,100},{124,116}... | collective-permute-start | bytes 7077896 | tf_op jit(solution)/shard_map/ppermute | solution.py:597
  34.1 32.8 %collective-permute-start.4 = (f32[2304,256]{1,0:T(8,128)S(1)}, f32[2304,256]{1,0:T(8,128)S(1)}, u32[]{:S(2)}, u32[]{:S(2)}) collective-permute-start(f32[2304,256]{1,0:T(8,128)S(1)} %shard_map.53.own), channel_id=1, source_target_pairs={{0,4},{8,12},{16,20},{24,28},{32,36},{40,44},{48,52},{56,60},{64,6... | collective-permute-start | bytes 7077896 | tf_op jit(solution)/shard_map/ppermute | solution.py:597
  52.1 8.6 %collective-permute-start.2 = (f32[1024,256]{1,0:T(8,128)S(1)}, f32[1024,256]{1,0:T(8,128)S(1)}, u32[]{:S(2)}, u32[]{:S(2)}) collective-permute-start(f32[1024,256]{1,0:T(8,128)S(1)} %get-tuple-element.16), channel_id=1, source_target_pairs={{0,4},{8,12},{16,20},{24,28},{32,36},{40,44},{48,52},{56,60},{64,6... | collective-permute-start | bytes 3145736 | tf_op jit(solution)/shard_map/ppermute | solution.py:597
  53.4 45.5 %collective-permute-start.6 = (f32[2304,256]{1,0:T(8,128)S(1)}, f32[2304,256]{1,0:T(8,128)S(1)}, u32[]{:S(2)}, u32[]{:S(2)}) collective-permute-start(f32[2304,256]{1,0:T(8,128)S(1)} %shard_map.53.own), channel_id=1, source_target_pairs={{8,4},{24,20},{40,36},{56,52},{72,68},{88,84},{104,100},{120,116},... | collective-permute-start | bytes 7077896 | tf_op jit(solution)/shard_map/ppermute | solution.py:597
  62.7 13.0 %collective-permute-start.3 = (f32[1024,256]{1,0:T(8,128)S(1)}, f32[1024,256]{1,0:T(8,128)S(1)}, u32[]{:S(2)}, u32[]{:S(2)}) collective-permute-start(f32[1024,256]{1,0:T(8,128)S(1)} %shard_map.52), channel_id=1, source_target_pairs={{4,12},{20,28},{36,44},{52,60},{68,76},{84,92},{100,108},{116,124}... | collective-permute-start | bytes 3145736 | tf_op jit(solution)/shard_map/ppermute | solution.py:597
  64.1 36.1 %collective-permute-start.10 = (f32[1024,256]{1,0:T(8,128)S(1)}, f32[1024,256]{1,0:T(8,128)S(1)}, u32[]{:S(2)}, u32[]{:S(2)}) collective-permute-start(f32[1024,256]{1,0:T(8,128)S(1)} %get-tuple-element.17.refs_2_.refs_4_.refs_7_.refs_17_.rhs), channel_id=1, source_target_pairs={{12,4},{4,12},{28,20},{20,28},{44,36},{36,44},{60,52},{52,60},{76,... | collective-permute-start | bytes 3145736 | tf_op jit(solution)/shard_map/ppermute | solution.py:597
  66.1 63.0 %collective-permute-start.14 = (f32[2304,256]{1,0:T(8,128)S(1)}, f32[2304,256]{1,0:T(8,128)S(1)}, u32[]{:S(2)}, u32[]{:S(2)}) collective-permute-start(f32[2304,256]{1,0:T(8,128)S(1)} %collective-permute-done.7.x), channel_id=1, source_target_pairs={{60,52},{92,84},{124,116},{61,53},{93,85},{125,117},{62,54},{94,86... | collective-permute-start | bytes 7077896 | tf_op jit(solution)/shard_map/ppermute | solution.py:597
  67.2 43.7 %collective-permute-start.15 = (f32[1152,256]{1,0:T(8,128)S(1)}, f32[1152,256]{1,0:T(8,128)S(1)}, u32[]{:S(2)}, u32[]{:S(2)}) collective-permute-start(f32[1152,256]{1,0:T(8,128)S(1)} %get-tuple-element.19), channel_id=1, source_target_pairs={{4,12},{20,28},{36,44},{52,60},{68,76},{84,92},{100,108},{116,124}... | collective-permute-start | bytes 3538952 | tf_op jit(solution)/shard_map/ppermute | solution.py:597
  75.7 36.2 %collective-permute-start.9 = (f32[1024,256]{1,0:T(8,128)S(1)}, f32[1024,256]{1,0:T(8,128)S(1)}, u32[]{:S(2)}, u32[]{:S(2)}) collective-permute-start(f32[1024,256]{1,0:T(8,128)S(1)} %get-tuple-element.17.refs_2_.refs_4_.refs_7_.refs_17_.rhs), channel_id=1, source_target_pairs={{8,4},{0,12},{24,20},{16,28},{40,36},{32,44},{56,52},{48,60},{72,6... | collective-permute-start | bytes 3145736 | tf_op jit(solution)/shard_map/ppermute | solution.py:597
  98.9 13.9 %collective-permute-start.8 = (f32[1024,256]{1,0:T(8,128)S(1)}, f32[1024,256]{1,0:T(8,128)S(1)}, u32[]{:S(2)}, u32[]{:S(2)}) collective-permute-start(f32[1024,256]{1,0:T(8,128)S(1)} %get-tuple-element.17.refs_2_.refs_4_.refs_7_.refs_17_.rhs), channel_id=1, source_target_pairs={{0,4},{16,20},{32,36},{48,52},{64,68},{80,84},{96,100},{112,116},{... | collective-permute-start | bytes 3145736 | tf_op jit(solution)/shard_map/ppermute | solution.py:597
  100.2 17.7 %collective-permute-start.5 = (f32[1024,256]{1,0:T(8,128)S(1)}, f32[1024,256]{1,0:T(8,128)S(1)}, u32[]{:S(2)}, u32[]{:S(2)}) collective-permute-start(f32[1024,256]{1,0:T(8,128)S(1)} %shard_map.55.ends.refs_22_), channel_id=1, source_target_pairs={{12,20},{28,36},{44,52},{60,68},{76,84},{92,100},{108,116},{13,21}... | collective-permute-start | bytes 3145736 | tf_op jit(solution)/shard_map/ppermute | solution.py:597
  110.9 28.2 %collective-permute-start.18 = (f32[1152,256]{1,0:T(8,128)S(1)}, f32[1152,256]{1,0:T(8,128)S(1)}, u32[]{:S(2)}, u32[]{:S(2)}) collective-permute-start(f32[1152,256]{1,0:T(8,128)S(1)} %collective-permute-done.15.p0), channel_id=1, source_target_pairs={{12,15},{13,12},{14,13},{15,14},{28,31},{29,28},{30,29},{31,30},{4... | collective-permute-start | bytes 3538952 | tf_op jit(solution)/shard_map/ppermute | solution.py:597
  111.9 36.5 %collective-permute-start.17 = (f32[1152,256]{1,0:T(8,128)S(1)}, f32[1152,256]{1,0:T(8,128)S(1)}, u32[]{:S(2)}, u32[]{:S(2)}) collective-permute-start(f32[1152,256]{1,0:T(8,128)S(1)} %collective-permute-done.15.p0), channel_id=1, source_target_pairs={{12,14},{13,15},{14,12},{15,13},{28,30},{29,31},{30,28},{31,29},{4... | collective-permute-start | bytes 3538952 | tf_op jit(solution)/shard_map/ppermute | solution.py:597
  112.8 35.6 %collective-permute-start.16 = (f32[1152,256]{1,0:T(8,128)S(1)}, f32[1152,256]{1,0:T(8,128)S(1)}, u32[]{:S(2)}, u32[]{:S(2)}) collective-permute-start(f32[1152,256]{1,0:T(8,128)S(1)} %collective-permute-done.15.p0), channel_id=1, source_target_pairs={{12,13},{13,14},{14,15},{15,12},{28,29},{29,30},{30,31},{31,28},{4... | collective-permute-start | bytes 3538952 | tf_op jit(solution)/shard_map/ppermute | solution.py:597
  126.1 22.8 %collective-permute-start.13 = (f32[1024,256]{1,0:T(8,128)S(1)}, f32[1024,256]{1,0:T(8,128)S(1)}, u32[]{:S(2)}, u32[]{:S(2)}) collective-permute-start(f32[1024,256]{1,0:T(8,128)S(1)} %shard_map.58.refs_8_.made.refs_19_), channel_id=1, source_target_pairs={{20,60},{4,12},{36,44},{68,76},{100,108},{21,61},{5,13},{37,45},{6... | collective-permute-start | bytes 3145736 | tf_op jit(solution)/shard_map/ppermute | solution.py:597
  129.1 21.7 %collective-permute-start.12 = (f32[1024,256]{1,0:T(8,128)S(1)}, f32[1024,256]{1,0:T(8,128)S(1)}, u32[]{:S(2)}, u32[]{:S(2)}) collective-permute-start(f32[1024,256]{1,0:T(8,128)S(1)} %shard_map.58.refs_8_.made.refs_19_), channel_id=1, source_target_pairs={{20,52},{36,60},{68,92},{100,124},{21,53},{37,61},{69,93},{101,125... | collective-permute-start | bytes 3145736 | tf_op jit(solution)/shard_map/ppermute | solution.py:597
  139.1 20.8 %collective-permute-start.11 = (f32[1024,256]{1,0:T(8,128)S(1)}, f32[1024,256]{1,0:T(8,128)S(1)}, u32[]{:S(2)}, u32[]{:S(2)}) collective-permute-start(f32[1024,256]{1,0:T(8,128)S(1)} %shard_map.58.refs_8_.made.refs_19_), channel_id=1, source_target_pairs={{36,52},{68,84},{100,116},{20,28},{52,60},{84,92},{116,124},{37,53... | collective-permute-start | bytes 3145736 | tf_op jit(solution)/shard_map/ppermute | solution.py:597
  161.6 2.0 collective-permute-start.20
  162.4 52.0 %collective-permute-start.22 = (f32[1024,256]{1,0:T(8,128)S(1)}, f32[1024,256]{1,0:T(8,128)S(1)}, u32[]{:S(2)}, u32[]{:S(2)}) collective-permute-start(f32[1024,256]{1,0:T(8,128)S(1)} %collective-permute-done.21.refs_6_), channel_id=1, source_target_pairs={{116,100},{117,101},{118,102},{119,103}} | collective-permute-start | bytes 3145736 | tf_op jit(solution)/shard_map/ppermute | solution.py:597
  217.8 8.7 %collective-permute-start.23 = (f32[1024,256]{1,0:T(8,128)S(1)}, f32[1024,256]{1,0:T(8,128)S(1)}, u32[]{:S(2)}, u32[]{:S(2)}) collective-permute-start(f32[1024,256]{1,0:T(8,128)S(1)} %get-tuple-element.26), channel_id=1, source_target_pairs={{4,0},{12,8},{20,16},{28,24},{36,32},{44,40},{52,48},{60,56},{68,6... | collective-permute-start | bytes 3145736 | tf_op jit(solution)/shard_map/ppermute | solution.py:597
  219.2 2.6 %collective-permute-start.24 = (f32[8,256]{1,0:T(8,128)S(1)}, f32[8,256]{1,0:T(8,128)S(1)}, u32[]{:S(2)}, u32[]{:S(2)}) collective-permute-start(f32[8,256]{1,0:T(8,128)S(1)} %get-tuple-element.29.a), channel_id=1, source_target_pairs={{0,1},{1,0},{2,3},{3,2},{4,5},{5,4},{6,7},{7,6},{8,9},{9,8},{10,11... | collective-permute-start | bytes 24584 | tf_op jit(solution)/shard_map/ppermute | solution.py:597
  221.8 4.0 %collective-permute-start.25 = (f32[8,256]{1,0:T(8,128)S(1)}, f32[8,256]{1,0:T(8,128)S(1)}, u32[]{:S(2)}, u32[]{:S(2)}) collective-permute-start(f32[8,256]{1,0:T(8,128)S(1)} %shard_map.67.a), channel_id=1, source_target_pairs={{0,2},{2,0},{1,3},{3,1},{4,6},{6,4},{5,7},{7,5},{8,10},{10,8},{9,1... | collective-permute-start | bytes 24584 | tf_op jit(solution)/shard_map/ppermute | solution.py:597
  (6 other events, 38.5 us)
